TPU v7x, 512 devices: a whole 4x8x8 slice. The times are simulated.
512 devices in a mesh: row: 32 (over z, x_hi, core), col: 16 (over y, x_lo).
Axes of the slice: x: 4 (x_hi: 2, x_lo: 2; x = x_hi * 2 + x_lo), y: 8, z: 8, core: 2. Of those that a mesh axis runs over, the one named last changes fastest.
Arguments:
- row_desc: bfloat16 [2048, 256, 256], P(('row', 'col')), may hold values from -32 to 32, as said below
- col_desc: bfloat16 [512, 256, 256], P(('row', 'col')), may hold values from -32 to 32, as said below
- col_coords: bfloat16 [512, 2, 256], P(('row', 'col')), may hold values from -1 to 1
- row_counts: int32 [2048], replicated, may hold values from 64 to 256
- col_counts: int32 [512], replicated, may hold values from 64 to 256
- row_cluster: int32 [2048], replicated, may hold values from 0 to 7
- col_cluster: int32 [512], replicated, may hold values from 0 to 7
Outputs:
- matches: float32 [6, 2048, 3, 256], P(None, ('row', 'col'))
Inputs may be any that keep to these rules, and one draw needn't show every extreme that they name: `row_desc`: custom descriptor draw. `col_desc`: custom descriptor draw.
All inputs are finite; a program needn't handle non-finite values.
Results may differ from a plain program's by a relative error of at most 0.0025.
Values may be sent and summed in bfloat16 or wider, within the bound.
No kernel may reach another device: no remote copies, remote signals or barrier semaphores. Data moves between devices by JAX's collectives and lax.ppermute only.
A program may use at most 64 MiB of HBM per device.

v0:
```python
import functools

import jax
import jax.numpy as jnp
from jax import lax
from jax.experimental import pallas as pl
from jax.experimental.pallas import tpu as pltpu
from jax.sharding import PartitionSpec as P


STEPS = 6
TABLE = 16
inv_temp = 10.0
big_value = 1e30

SMEM = pl.BlockSpec(memory_space=pltpu.SMEM)
VMEM = pl.BlockSpec(memory_space=pltpu.VMEM)


def shift(value, by_row, by_col):
    n_row, n_col = lax.axis_size("row"), lax.axis_size("col")
    perm = [
        (i * n_col + j, (i + by_row) % n_row * n_col + (j + by_col) % n_col)
        for i in range(n_row)
        for j in range(n_col)
    ]
    return lax.ppermute(value, ("row", "col"), perm)


def one_pair(rows, packed, row_count, col_count):
    k = packed.shape[0] - TABLE
    scores = inv_temp * lax.dot_general(
        packed[:k], rows, (((1,), (1,)), ((), ())), preferred_element_type=jnp.float32
    )
    col_ok = lax.broadcasted_iota(jnp.int32, scores.shape, 0) < col_count
    row_ok = lax.broadcasted_iota(jnp.int32, scores.shape, 1) < row_count
    over_col = jnp.where(col_ok, scores, -big_value)
    over_row = jnp.where(row_ok, scores, -big_value)
    row_exp = jnp.exp(over_col - jnp.max(over_col, axis=0, keepdims=True))
    col_exp = jnp.exp(over_row - jnp.max(over_row, axis=1, keepdims=True))
    row_inv = 1.0 / jnp.sum(row_exp, axis=0, keepdims=True)
    col_inv = 1.0 / jnp.sum(col_exp, axis=1, keepdims=True)
    prob = ((row_exp * row_inv) * (col_exp * col_inv)).astype(jnp.bfloat16)
    return lax.dot_general(
        packed[k:], prob, (((1,), (0,)), ((), ())), preferred_element_type=jnp.float32
    )


def panel(step, rows_ref, packed_ref, meta_ref, out_ref):
    out_ref[...] = jnp.zeros_like(out_ref)

    def body(r, carry):
        at = (step * rows_ref.shape[0] + r) * 4

        @pl.when(meta_ref[at] == 1)
        def _():
            found = one_pair(
                rows_ref[r], packed_ref[...], meta_ref[at + 1], meta_ref[at + 2]
            )
            for c in range(3):
                out_ref[c, pl.ds(r, 1), :] = found[c : c + 1]

        return carry

    lax.fori_loop(0, rows_ref.shape[0], body, 0)


def pack_kernel(col_desc, coords, packed, table_in, sems):
    k = col_desc.shape[1]
    copies = [
        pltpu.make_async_copy(coords, table_in, sems.at[0]),
        pltpu.make_async_copy(col_desc, packed.at[:, :k], sems.at[1]),
    ]
    for copy in copies:
        copy.start()
    copies[0].wait()
    at = lax.broadcasted_iota(jnp.int32, (TABLE, k), 0)
    x = table_in[0, 0:1].astype(jnp.float32)
    y = table_in[0, 1:2].astype(jnp.float32)
    zero = jnp.zeros((TABLE, k), jnp.float32)
    table = jnp.where(at == 0, 1.0, jnp.where(at == 1, x, jnp.where(at == 2, y, zero)))
    table = table.astype(jnp.bfloat16)
    packed[0, k:] = table
    copies[1].wait()


def join_kernel(image2, image4, out):
    out[0] = image2[0]
    out[1] = image4[0]


def first_kernel(
    sizes, row_counts, col_counts, row_cluster, col_cluster, rows, packed, out, meta
):
    n_row, n_col = sizes
    ri = rows.shape[0]
    row_pos, col_pos = lax.axis_index("row"), lax.axis_index("col")
    for step in range(STEPS):
        odd = step % 2
        block = row_pos * n_col + lax.rem(col_pos - (step - odd) + n_col, n_col)
        image = lax.rem(row_pos - step + n_row, n_row) * n_col + lax.rem(col_pos + odd, n_col)
        for r in range(ri):
            at = (step * ri + r) * 4
            same = row_cluster[block * ri + r] == col_cluster[image]
            meta[at] = same.astype(jnp.int32)
            meta[at + 1] = row_counts[block * ri + r]
            meta[at + 2] = col_counts[image]
            meta[at + 3] = 0
    panel(0, rows, packed.at[0], meta, out)


def second_kernel(meta, rows, packed, out):
    panel(2, rows, packed.at[0], meta, out)


def odd_kernel(meta, rows0, rows2, rows4, image1, images, out):
    panel(1, rows0, image1.at[0], meta, out.at[0])
    panel(3, rows2, images.at[0], meta, out.at[1])
    panel(5, rows4, images.at[1], meta, out.at[2])


def fourth_kernel(meta, rows, packed, out):
    panel(4, rows, packed.at[0], meta, out)


def final_kernel(res0, res2, res4, home, out, sems):
    copies = [
        pltpu.make_async_copy(home.at[n], out.at[2 * n + 1], sems.at[n]) for n in range(3)
    ] + [
        pltpu.make_async_copy(res, out.at[2 * n], sems.at[3 + n])
        for n, res in enumerate((res0, res2, res4))
    ]
    for copy in copies:
        copy.start()
    for copy in copies:
        copy.wait()


def near(value):
    return pltpu.with_memory_space_constraint(value, pltpu.VMEM)


def local(row_desc, col_desc, col_coords, row_counts, col_counts, row_cluster, col_cluster):
    n_row, n_col = lax.axis_size("row"), lax.axis_size("col")
    ri, slots, depth = row_desc.shape
    k = slots + TABLE

    def many(*count):
        return pltpu.VMEM((*count, 3, ri, slots), jnp.float32)

    rows2 = shift(row_desc, 0, 2)
    packed = pl.pallas_call(
        pack_kernel,
        out_shape=pltpu.VMEM((1, k, depth), jnp.bfloat16),
        in_specs=[pl.BlockSpec(memory_space=pl.ANY)] * 2,
        out_specs=VMEM,
        scratch_shapes=[
            pltpu.VMEM(col_coords.shape, jnp.bfloat16),
            pltpu.SemaphoreType.DMA((2,)),
        ],
        name="pack",
    )(col_desc, col_coords)
    image2 = shift(packed, 2, 0)
    image4 = shift(packed, 4, 0)
    rows4 = shift(rows2, 0, 2)
    joined = pl.pallas_call(
        join_kernel,
        out_shape=pltpu.VMEM((2, k, depth), jnp.bfloat16),
        in_specs=[VMEM] * 2,
        out_specs=VMEM,
        name="join",
    )(near(image2), near(image4))
    images35 = shift(joined, 1, -1)
    image1 = shift(packed, 1, -1)
    rows0 = near(row_desc)

    res0, meta = pl.pallas_call(
        functools.partial(first_kernel, (n_row, n_col)),
        out_shape=(many(), jax.ShapeDtypeStruct((STEPS * ri * 4,), jnp.int32)),
        in_specs=[SMEM] * 4 + [VMEM] * 2,
        out_specs=(VMEM, SMEM),
        name="first",
    )(row_counts, col_counts, row_cluster, col_cluster, rows0, near(packed))
    res2 = pl.pallas_call(
        second_kernel,
        out_shape=many(),
        in_specs=[SMEM] + [VMEM] * 2,
        out_specs=VMEM,
        name="second",
    )(meta, near(rows2), near(image2))
    res135 = pl.pallas_call(
        odd_kernel,
        out_shape=many(3),
        in_specs=[SMEM] + [VMEM] * 5,
        out_specs=VMEM,
        name="odd",
    )(meta, rows0, near(rows2), near(rows4), near(image1), near(images35))
    home = shift(res135, 0, 1)
    res4 = pl.pallas_call(
        fourth_kernel,
        out_shape=many(),
        in_specs=[SMEM] + [VMEM] * 2,
        out_specs=VMEM,
        name="fourth",
    )(meta, near(rows4), near(image4))
    done = pl.pallas_call(
        final_kernel,
        out_shape=jax.ShapeDtypeStruct((STEPS, 3, ri, slots), jnp.float32),
        in_specs=[VMEM] * 4,
        out_specs=pl.BlockSpec(memory_space=pl.ANY),
        scratch_shapes=[pltpu.SemaphoreType.DMA((6,))],
        name="final",
    )(near(res0), near(res2), near(res4), near(home))
    return jnp.transpose(done, (0, 2, 1, 3))


def solution(mesh):
    return jax.shard_map(
        local,
        mesh=mesh,
        in_specs=(
            P(("row", "col"), None, None),
            P(("row", "col"), None, None),
            P(("row", "col"), None, None),
            P(),
            P(),
            P(),
            P(),
        ),
        out_specs=P(None, ("row", "col"), None, None),
        check_vma=False,
    )
```

profile of v0, /device:TPU:24, one launch (start us, length us, event | category | flops | bytes accessed | tf_op | source)
XLA Modules:
  0.0 65.6 jit_solution(7994286564105919301)
XLA Ops:
  0.0 0.0 copy-start
  0.0 4.8 %collective-permute-start = (bf16[4,256,256]{2,1,0:T(8,128)(2,1)}, bf16[4,256,256]{2,1,0:T(8,128)(2,1)S(1)}, u32[]{:S(2)}, u32[]{:S(2)}) collective-permute-start(bf16[4,256,256]{2,1,0:T(8,128)(2,1)} %rows0.1), channel_id=1, source_target_pairs={{0,2},{1,3},{2,4},{3,5},{4,6},{5,7},{6,8},{7,9},{8,10},{9,11},{10,... | collective-permute-start | bytes 1572872 | tf_op jit(solution)/shard_map/ppermute | solution.py:27
  4.8 11.5 %collective-permute-done.rows.rows2 = bf16[4,256,256]{2,1,0:T(8,128)(2,1)S(1)} collective-permute-done((bf16[4,256,256]{2,1,0:T(8,128)(2,1)}, bf16[4,256,256]{2,1,0:T(8,128)(2,1)S(1)}, u32[]{:S(2)}, u32[]{:S(2)}) %collective-permute-start) | collective-permute-done | bytes 524320 | tf_op jit(solution)/shard_map/ppermute | solution.py:27
  16.3 5.5 %collective-permute-start.2 = (bf16[4,256,256]{2,1,0:T(8,128)(2,1)S(1)}, bf16[4,256,256]{2,1,0:T(8,128)(2,1)S(1)}, u32[]{:S(2)}, u32[]{:S(2)}) collective-permute-start(bf16[4,256,256]{2,1,0:T(8,128)(2,1)S(1)} %collective-permute-done.rows.rows2), channel_id=1, source_target_pairs={{0,2},{1,3},{2,4},{3,5},{4,6},{5,7},{6,8},{7,9},{8,10},{9,11},{10,... | collective-permute-start | bytes 1572872 | tf_op jit(solution)/shard_map/ppermute | solution.py:27
  21.8 0.9 %pack.1.packed = bf16[1,272,256]{2,1,0:T(8,128)(2,1)S(1)} custom-call(bf16[1,256,256]{2,1,0:T(8,128)(2,1)} %col_desc.1, bf16[1,2,256]{2,1,0:T(2,128)(2,1)} %coords.1), custom_call_target="tpu_custom_call" | custom-call | tf_op jit(solution)/shard_map/pack/pallas_call | solution.py:152
  22.7 4.3 %collective-permute-start.3 = (bf16[1,272,256]{2,1,0:T(8,128)(2,1)S(1)}, bf16[1,272,256]{2,1,0:T(8,128)(2,1)S(1)}, u32[]{:S(2)}, u32[]{:S(2)}) collective-permute-start(bf16[1,272,256]{2,1,0:T(8,128)(2,1)S(1)} %pack.1.packed), channel_id=1, source_target_pairs={{0,64},{1,65},{2,66},{3,67},{4,68},{5,69},{6,70},{7,71},{8,72},{9,... | collective-permute-start | bytes 417800 | tf_op jit(solution)/shard_map/ppermute | solution.py:27
  27.0 4.9 %collective-permute-start.1 = (bf16[1,272,256]{2,1,0:T(8,128)(2,1)S(1)}, bf16[1,272,256]{2,1,0:T(8,128)(2,1)S(1)}, u32[]{:S(2)}, u32[]{:S(2)}) collective-permute-start(bf16[1,272,256]{2,1,0:T(8,128)(2,1)S(1)} %pack.1.packed), channel_id=1, source_target_pairs={{0,32},{1,33},{2,34},{3,35},{4,36},{5,37},{6,38},{7,39},{8,40},{9,... | collective-permute-start | bytes 417800 | tf_op jit(solution)/shard_map/ppermute | solution.py:27
  32.0 4.8 %collective-permute-done.3.packed.image4 = bf16[1,272,256]{2,1,0:T(8,128)(2,1)S(1)} collective-permute-done((bf16[1,272,256]{2,1,0:T(8,128)(2,1)S(1)}, bf16[1,272,256]{2,1,0:T(8,128)(2,1)S(1)}, u32[]{:S(2)}, u32[]{:S(2)}) %collective-permute-start.3) | collective-permute-done | bytes 139296 | tf_op jit(solution)/shard_map/ppermute | solution.py:27
  36.7 5.4 %collective-permute-done.1.packed.image2 = bf16[1,272,256]{2,1,0:T(8,128)(2,1)S(1)} collective-permute-done((bf16[1,272,256]{2,1,0:T(8,128)(2,1)S(1)}, bf16[1,272,256]{2,1,0:T(8,128)(2,1)S(1)}, u32[]{:S(2)}, u32[]{:S(2)}) %collective-permute-start.1) | collective-permute-done | bytes 139296 | tf_op jit(solution)/shard_map/ppermute | solution.py:27
  42.1 1.9 %collective-permute-start.5 = (bf16[2,272,256]{2,1,0:T(8,128)(2,1)S(1)}, bf16[2,272,256]{2,1,0:T(8,128)(2,1)S(1)}, u32[]{:S(2)}, u32[]{:S(2)}) collective-permute-start(bf16[2,272,256]{2,1,0:T(8,128)(2,1)S(1)} %join.1), channel_id=1, source_target_pairs={{0,31},{1,16},{2,17},{3,18},{4,19},{5,20},{6,21},{7,22},{8,23},{9,... | collective-permute-start | bytes 835592 | tf_op jit(solution)/shard_map/ppermute | solution.py:27
  44.1 1.9 %collective-permute-start.4 = (bf16[1,272,256]{2,1,0:T(8,128)(2,1)S(1)}, bf16[1,272,256]{2,1,0:T(8,128)(2,1)S(1)}, u32[]{:S(2)}, u32[]{:S(2)}) collective-permute-start(bf16[1,272,256]{2,1,0:T(8,128)(2,1)S(1)} %pack.1.packed), channel_id=1, source_target_pairs={{0,31},{1,16},{2,17},{3,18},{4,19},{5,20},{6,21},{7,22},{8,23},{9,... | collective-permute-start | bytes 417800 | tf_op jit(solution)/shard_map/ppermute | solution.py:27
  46.0 0.0 copy-done
  46.0 1.7 %first.1 = (f32[3,4,256]{2,1,0:T(4,128)S(1)}, s32[96]{0:T(128)}) custom-call(s32[2048]{0:T(1024)} %row_counts.1, s32[512]{0:T(512)} %col_counts.1, s32[2048]{0:T(1024)} %row_cluster.1, s32[512]{0:T(512)} %col_cluster.1, bf16[4,256,256]{2,1,0:T(8,128)(2,1)S(1)} %copy-done, bf16[1,272,256]{2,1,0:T(8,128)(2,1)S(1)} %pack.1.packed), custom_call_target="tpu_custom_call" | custom-call | tf_op jit(solution)/shard_map/first/pallas_call | solution.py:177
  47.7 7.1 %collective-permute-done.4.image1 = bf16[1,272,256]{2,1,0:T(8,128)(2,1)S(1)} collective-permute-done((bf16[1,272,256]{2,1,0:T(8,128)(2,1)S(1)}, bf16[1,272,256]{2,1,0:T(8,128)(2,1)S(1)}, u32[]{:S(2)}, u32[]{:S(2)}) %collective-permute-start.4) | collective-permute-done | bytes 139296 | tf_op jit(solution)/shard_map/ppermute | solution.py:27
  54.8 0.0 collective-permute-done.5.images
  54.8 0.0 collective-permute-done.2.rows.rows4
  54.8 3.4 %odd.1 = f32[3,3,4,256]{3,2,1,0:T(4,128)S(1)} custom-call(s32[96]{0:T(128)} %get-tuple-element.8.meta, bf16[4,256,256]{2,1,0:T(8,128)(2,1)S(1)} %copy-done, bf16[4,256,256]{2,1,0:T(8,128)(2,1)S(1)} %collective-permute-done.rows.rows2, bf16[4,256,256]{2,1,0:T(8,128)(2,1)S(1)} %collective-permute-done.2.rows.rows4, ...), custom_call_target="tpu_custom_call" | custom-call | tf_op jit(solution)/shard_map/odd/pallas_call | solution.py:191
  58.2 1.9 %collective-permute-start.6 = (f32[3,3,4,256]{3,2,1,0:T(4,128)S(1)}, f32[3,3,4,256]{3,2,1,0:T(4,128)S(1)}, u32[]{:S(2)}, u32[]{:S(2)}) collective-permute-start(f32[3,3,4,256]{3,2,1,0:T(4,128)S(1)} %odd.1), channel_id=1, source_target_pairs={{0,1},{1,2},{2,3},{3,4},{4,5},{5,6},{6,7},{7,8},{8,9},{9,10},{10,1... | collective-permute-start | bytes 110600 | tf_op jit(solution)/shard_map/ppermute | solution.py:27
  60.1 1.2 %second.1.res2 = f32[3,4,256]{2,1,0:T(4,128)S(1)} custom-call(s32[96]{0:T(128)} %get-tuple-element.8.meta, bf16[4,256,256]{2,1,0:T(8,128)(2,1)S(1)} %collective-permute-done.rows.rows2, bf16[1,272,256]{2,1,0:T(8,128)(2,1)S(1)} %collective-permute-done.1.packed.image2), custom_call_target="tpu_custom_call" | custom-call | tf_op jit(solution)/shard_map/second/pallas_call | solution.py:184
  61.4 1.8 %fourth.1.res4 = f32[3,4,256]{2,1,0:T(4,128)S(1)} custom-call(s32[96]{0:T(128)} %get-tuple-element.8.meta, bf16[4,256,256]{2,1,0:T(8,128)(2,1)S(1)} %collective-permute-done.2.rows.rows4, bf16[1,272,256]{2,1,0:T(8,128)(2,1)S(1)} %collective-permute-done.3.packed.image4), custom_call_target="tpu_custom_call" | custom-call | tf_op jit(solution)/shard_map/fourth/pallas_call | solution.py:199
  63.1 1.8 %collective-permute-done.6.home = f32[3,3,4,256]{3,2,1,0:T(4,128)S(1)} collective-permute-done((f32[3,3,4,256]{3,2,1,0:T(4,128)S(1)}, f32[3,3,4,256]{3,2,1,0:T(4,128)S(1)}, u32[]{:S(2)}, u32[]{:S(2)}) %collective-permute-start.6) | collective-permute-done | bytes 36896 | tf_op jit(solution)/shard_map/ppermute | solution.py:27
  65.0 0.7 %final.1 = f32[6,3,4,256]{3,2,1,0:T(4,128)} custom-call(f32[3,4,256]{2,1,0:T(4,128)S(1)} %get-tuple-element.7.res0, f32[3,4,256]{2,1,0:T(4,128)S(1)} %second.1.res2, f32[3,4,256]{2,1,0:T(4,128)S(1)} %fourth.1.res4, f32[3,3,4,256]{3,2,1,0:T(4,128)S(1)} %collective-permute-done.6.home), custom_call_target="tpu_custom_call" | custom-call | tf_op jit(solution)/shard_map/final/pallas_call | solution.py:206
  (1 shorter events, 0.0 us)
Async XLA Ops:
  0.0 46.0 %copy-start = (bf16[4,256,256]{2,1,0:T(8,128)(2,1)S(1)}, bf16[4,256,256]{2,1,0:T(8,128)(2,1)}, u32[]{:S(2)}) copy-start(bf16[4,256,256]{2,1,0:T(8,128)(2,1)} %rows0.1) | copy-start | bytes 1572868
  0.0 16.3 %collective-permute-start = (bf16[4,256,256]{2,1,0:T(8,128)(2,1)}, bf16[4,256,256]{2,1,0:T(8,128)(2,1)S(1)}, u32[]{:S(2)}, u32[]{:S(2)}) collective-permute-start(bf16[4,256,256]{2,1,0:T(8,128)(2,1)} %rows0.1), channel_id=1, source_target_pairs={{0,2},{1,3},{2,4},{3,5},{4,6},{5,7},{6,8},{7,9},{8,10},{9,11},{10,... | collective-permute-start | bytes 1572872 | tf_op jit(solution)/shard_map/ppermute | solution.py:27
  16.3 38.5 %collective-permute-start.2 = (bf16[4,256,256]{2,1,0:T(8,128)(2,1)S(1)}, bf16[4,256,256]{2,1,0:T(8,128)(2,1)S(1)}, u32[]{:S(2)}, u32[]{:S(2)}) collective-permute-start(bf16[4,256,256]{2,1,0:T(8,128)(2,1)S(1)} %collective-permute-done.rows.rows2), channel_id=1, source_target_pairs={{0,2},{1,3},{2,4},{3,5},{4,6},{5,7},{6,8},{7,9},{8,10},{9,11},{10,... | collective-permute-start | bytes 1572872 | tf_op jit(solution)/shard_map/ppermute | solution.py:27
  22.7 14.0 %collective-permute-start.3 = (bf16[1,272,256]{2,1,0:T(8,128)(2,1)S(1)}, bf16[1,272,256]{2,1,0:T(8,128)(2,1)S(1)}, u32[]{:S(2)}, u32[]{:S(2)}) collective-permute-start(bf16[1,272,256]{2,1,0:T(8,128)(2,1)S(1)} %pack.1.packed), channel_id=1, source_target_pairs={{0,64},{1,65},{2,66},{3,67},{4,68},{5,69},{6,70},{7,71},{8,72},{9,... | collective-permute-start | bytes 417800 | tf_op jit(solution)/shard_map/ppermute | solution.py:27
  27.0 15.1 %collective-permute-start.1 = (bf16[1,272,256]{2,1,0:T(8,128)(2,1)S(1)}, bf16[1,272,256]{2,1,0:T(8,128)(2,1)S(1)}, u32[]{:S(2)}, u32[]{:S(2)}) collective-permute-start(bf16[1,272,256]{2,1,0:T(8,128)(2,1)S(1)} %pack.1.packed), channel_id=1, source_target_pairs={{0,32},{1,33},{2,34},{3,35},{4,36},{5,37},{6,38},{7,39},{8,40},{9,... | collective-permute-start | bytes 417800 | tf_op jit(solution)/shard_map/ppermute | solution.py:27
  42.1 12.7 %collective-permute-start.5 = (bf16[2,272,256]{2,1,0:T(8,128)(2,1)S(1)}, bf16[2,272,256]{2,1,0:T(8,128)(2,1)S(1)}, u32[]{:S(2)}, u32[]{:S(2)}) collective-permute-start(bf16[2,272,256]{2,1,0:T(8,128)(2,1)S(1)} %join.1), channel_id=1, source_target_pairs={{0,31},{1,16},{2,17},{3,18},{4,19},{5,20},{6,21},{7,22},{8,23},{9,... | collective-permute-start | bytes 835592 | tf_op jit(solution)/shard_map/ppermute | solution.py:27
  44.1 10.8 %collective-permute-start.4 = (bf16[1,272,256]{2,1,0:T(8,128)(2,1)S(1)}, bf16[1,272,256]{2,1,0:T(8,128)(2,1)S(1)}, u32[]{:S(2)}, u32[]{:S(2)}) collective-permute-start(bf16[1,272,256]{2,1,0:T(8,128)(2,1)S(1)} %pack.1.packed), channel_id=1, source_target_pairs={{0,31},{1,16},{2,17},{3,18},{4,19},{5,20},{6,21},{7,22},{8,23},{9,... | collective-permute-start | bytes 417800 | tf_op jit(solution)/shard_map/ppermute | solution.py:27
  58.2 6.7 %collective-permute-start.6 = (f32[3,3,4,256]{3,2,1,0:T(4,128)S(1)}, f32[3,3,4,256]{3,2,1,0:T(4,128)S(1)}, u32[]{:S(2)}, u32[]{:S(2)}) collective-permute-start(f32[3,3,4,256]{3,2,1,0:T(4,128)S(1)} %odd.1), channel_id=1, source_target_pairs={{0,1},{1,2},{2,3},{3,4},{4,5},{5,6},{6,7},{7,8},{8,9},{9,10},{10,1... | collective-permute-start | bytes 110600 | tf_op jit(solution)/shard_map/ppermute | solution.py:27
where the time goes:
time: 66 us; the launch traced here: 65.6 us
  waiting for transfers between devices  30.5 us (46%)
  starting transfers between devices  25.3 us (38%)
  Pallas kernels  9.73 us (15%)
    ppermute x7, waiting for transfers between devices, shift(): return lax.ppermute(value, ('row', 'col'), perm)  30.5 us
    ppermute x7, starting transfers between devices, shift(): return lax.ppermute(value, ('row', 'col'), perm)  25.3 us
    pallas_call x1, Pallas kernels, local(): pl.pallas_call(odd_kernel, out_shape=many(3), in_specs=[SMEM] + [VMEM] *...  3.39 us
    pallas_call x1, Pallas kernels, local(): pl.pallas_call(fourth_kernel, out_shape=many(), in_specs=[SMEM] + [VMEM]...  1.77 us
    pallas_call x1, Pallas kernels, local(): pl.pallas_call(functools.partial(first_kernel, (n_row, n_col)), out_shape...  1.69 us
  transfers between devices with their start and end apart: 7, of which 5 were waited for; matrix products, arithmetic and copies ran while one was open for 0% of the time, Pallas kernels for 9%

commit v1 on v0

--- a/solution.py
+++ b/solution.py
@@ -10,6 +10,8 @@
 
 STEPS = 6
 TABLE = 16
+COLS = 24
+FLAGS = 32
 inv_temp = 10.0
 big_value = 1e30
 
@@ -17,14 +19,18 @@
 VMEM = pl.BlockSpec(memory_space=pltpu.VMEM)
 
 
-def shift(value, by_row, by_col):
+def move(value, target, by_col):
     n_row, n_col = lax.axis_size("row"), lax.axis_size("col")
     perm = [
-        (i * n_col + j, (i + by_row) % n_row * n_col + (j + by_col) % n_col)
+        (i * n_col + j, target(i) % n_row * n_col + (j + by_col) % n_col)
         for i in range(n_row)
         for j in range(n_col)
     ]
     return lax.ppermute(value, ("row", "col"), perm)
+
+
+def shift(value, by_row, by_col):
+    return move(value, lambda i: i + by_row, by_col)
 
 
 def one_pair(rows, packed, row_count, col_count):
@@ -33,7 +39,7 @@
         packed[:k], rows, (((1,), (1,)), ((), ())), preferred_element_type=jnp.float32
     )
     col_ok = lax.broadcasted_iota(jnp.int32, scores.shape, 0) < col_count
-    row_ok = lax.broadcasted_iota(jnp.int32, scores.shape, 1) < row_count
+    row_ok = lax.broadcasted_iota(jnp.int32, (1, scores.shape[1]), 1) < row_count
     over_col = jnp.where(col_ok, scores, -big_value)
     over_row = jnp.where(row_ok, scores, -big_value)
     row_exp = jnp.exp(over_col - jnp.max(over_col, axis=0, keepdims=True))
@@ -47,22 +53,27 @@
 
 
 def panel(step, rows_ref, packed_ref, meta_ref, out_ref):
+    ri = rows_ref.shape[0]
     out_ref[...] = jnp.zeros_like(out_ref)
+    flags = jnp.max(meta_ref[pl.ds(FLAGS + step, 1), :].astype(jnp.float32)).astype(jnp.int32)
 
     def body(r, carry):
-        at = (step * rows_ref.shape[0] + r) * 4
-
-        @pl.when(meta_ref[at] == 1)
+        @pl.when(((flags >> r) & 1) == 1)
         def _():
             found = one_pair(
-                rows_ref[r], packed_ref[...], meta_ref[at + 1], meta_ref[at + 2]
+                rows_ref[r],
+                packed_ref[...],
+                meta_ref[pl.ds(step * ri + r, 1), :],
+                meta_ref[pl.ds(COLS + step, 1), :],
             )
             for c in range(3):
                 out_ref[c, pl.ds(r, 1), :] = found[c : c + 1]
 
         return carry
 
-    lax.fori_loop(0, rows_ref.shape[0], body, 0)
+    @pl.when(flags != 0)
+    def _():
+        lax.fori_loop(0, ri, body, 0)
 
 
 def pack_kernel(col_desc, coords, packed, table_in, sems):
@@ -95,17 +106,20 @@
     n_row, n_col = sizes
     ri = rows.shape[0]
     row_pos, col_pos = lax.axis_index("row"), lax.axis_index("col")
+    slots = rows.shape[1]
     for step in range(STEPS):
         odd = step % 2
         block = row_pos * n_col + lax.rem(col_pos - (step - odd) + n_col, n_col)
         image = lax.rem(row_pos - step + n_row, n_row) * n_col + lax.rem(col_pos + odd, n_col)
+        flags = 0
         for r in range(ri):
-            at = (step * ri + r) * 4
             same = row_cluster[block * ri + r] == col_cluster[image]
-            meta[at] = same.astype(jnp.int32)
-            meta[at + 1] = row_counts[block * ri + r]
-            meta[at + 2] = col_counts[image]
-            meta[at + 3] = 0
+            flags += same.astype(jnp.int32) * (1 << r)
+            meta[pl.ds(step * ri + r, 1), :] = jnp.full(
+                (1, slots), row_counts[block * ri + r], jnp.int32
+            )
+        meta[pl.ds(COLS + step, 1), :] = jnp.full((1, slots), col_counts[image], jnp.int32)
+        meta[pl.ds(FLAGS + step, 1), :] = jnp.full((1, slots), flags, jnp.int32)
     panel(0, rows, packed.at[0], meta, out)
 
 
@@ -113,10 +127,20 @@
     panel(2, rows, packed.at[0], meta, out)
 
 
-def odd_kernel(meta, rows0, rows2, rows4, image1, images, out):
-    panel(1, rows0, image1.at[0], meta, out.at[0])
-    panel(3, rows2, images.at[0], meta, out.at[1])
-    panel(5, rows4, images.at[1], meta, out.at[2])
+def odd_kernel(meta, rows0, rows2, rows4, direct, images, out):
+    even_row = lax.rem(lax.axis_index("row"), 2) == 0
+
+    @pl.when(even_row)
+    def _():
+        panel(1, rows0, images.at[0], meta, out.at[0])
+        panel(3, rows2, images.at[1], meta, out.at[1])
+        panel(5, rows4, direct.at[0], meta, out.at[2])
+
+    @pl.when(jnp.logical_not(even_row))
+    def _():
+        panel(1, rows0, direct.at[0], meta, out.at[0])
+        panel(3, rows2, images.at[0], meta, out.at[1])
+        panel(5, rows4, images.at[1], meta, out.at[2])
 
 
 def fourth_kernel(meta, rows, packed, out):
@@ -170,39 +194,39 @@
         out_specs=VMEM,
         name="join",
     )(near(image2), near(image4))
-    images35 = shift(joined, 1, -1)
-    image1 = shift(packed, 1, -1)
+    images = move(joined, lambda i: i ^ 1, -1)
+    direct = move(packed, lambda i: i + (5 if i % 2 else 1), -1)
     rows0 = near(row_desc)
 
     res0, meta = pl.pallas_call(
         functools.partial(first_kernel, (n_row, n_col)),
-        out_shape=(many(), jax.ShapeDtypeStruct((STEPS * ri * 4,), jnp.int32)),
+        out_shape=(many(), pltpu.VMEM((FLAGS + 8, slots), jnp.int32)),
         in_specs=[SMEM] * 4 + [VMEM] * 2,
-        out_specs=(VMEM, SMEM),
+        out_specs=(VMEM, VMEM),
         name="first",
     )(row_counts, col_counts, row_cluster, col_cluster, rows0, near(packed))
     res2 = pl.pallas_call(
         second_kernel,
         out_shape=many(),
-        in_specs=[SMEM] + [VMEM] * 2,
+        in_specs=[VMEM] * 3,
         out_specs=VMEM,
         name="second",
-    )(meta, near(rows2), near(image2))
+    )(near(meta), near(rows2), near(image2))
     res135 = pl.pallas_call(
         odd_kernel,
         out_shape=many(3),
-        in_specs=[SMEM] + [VMEM] * 5,
+        in_specs=[VMEM] * 6,
         out_specs=VMEM,
         name="odd",
-    )(meta, rows0, near(rows2), near(rows4), near(image1), near(images35))
+    )(near(meta), rows0, near(rows2), near(rows4), near(direct), near(images))
     home = shift(res135, 0, 1)
     res4 = pl.pallas_call(
         fourth_kernel,
         out_shape=many(),
-        in_specs=[SMEM] + [VMEM] * 2,
+        in_specs=[VMEM] * 3,
         out_specs=VMEM,
         name="fourth",
-    )(meta, near(rows4), near(image4))
+    )(near(meta), near(rows4), near(image4))
     done = pl.pallas_call(
         final_kernel,
         out_shape=jax.ShapeDtypeStruct((STEPS, 3, ri, slots), jnp.float32),

time: 66 us -> 67 us (1.015)
  waiting for transfers between devices: 30.5 us -> 33.4 us
  Pallas kernels: 9.73 us -> 7.83 us
    ppermute x7, waiting for transfers between devices: 30.5 us -> 33.4 us  [move(): return lax.ppermute(value, ('row', 'col'), perm)]
    pallas_call x3, Pallas kernels: 6.41 us -> 5.05 us  [the longest x1 3.13 us: local(): pl.pallas_call(odd_kernel, out_shape=many(3), in_specs=[VMEM] * 6, out_sp...]
  transfers between devices with their start and end apart: 7 -> 7, of which waited for: 5 -> 5; matrix products, arithmetic and copies ran while one was open for 0% -> 0% of each run, Pallas kernels for 9% -> 6%
where the time goes in v1:
time: 67 us; the launch traced here: 66.7 us
  waiting for transfers between devices  33.4 us (50%)
  starting transfers between devices  25.3 us (38%)
  Pallas kernels  7.83 us (12%)
    ppermute x7, waiting for transfers between devices, move(): return lax.ppermute(value, ('row', 'col'), perm)  33.4 us
    ppermute x7, starting transfers between devices, move(): return lax.ppermute(value, ('row', 'col'), perm)  25.3 us
    pallas_call x1, Pallas kernels, local(): pl.pallas_call(odd_kernel, out_shape=many(3), in_specs=[VMEM] * 6, out_sp...  3.13 us
  transfers between devices with their start and end apart: 7, of which 5 were waited for; matrix products, arithmetic and copies ran while one was open for 0% of the time, Pallas kernels for 6%

profile of v1, /device:TPU:24, one launch (start us, length us, event | category | flops | bytes accessed | tf_op | source)
XLA Modules:
  0.0 66.7 jit_solution(16578648313579546465)
XLA Ops:
  0.0 0.0 copy-start
  0.0 4.8 %collective-permute-start = (bf16[4,256,256]{2,1,0:T(8,128)(2,1)}, bf16[4,256,256]{2,1,0:T(8,128)(2,1)S(1)}, u32[]{:S(2)}, u32[]{:S(2)}) collective-permute-start(bf16[4,256,256]{2,1,0:T(8,128)(2,1)} %rows0.1), channel_id=1, source_target_pairs={{0,2},{1,3},{2,4},{3,5},{4,6},{5,7},{6,8},{7,9},{8,10},{9,11},{10,... | collective-permute-start | bytes 1572872 | tf_op jit(solution)/shard_map/ppermute | solution.py:29
  4.8 11.5 %collective-permute-done.rows.rows2 = bf16[4,256,256]{2,1,0:T(8,128)(2,1)S(1)} collective-permute-done((bf16[4,256,256]{2,1,0:T(8,128)(2,1)}, bf16[4,256,256]{2,1,0:T(8,128)(2,1)S(1)}, u32[]{:S(2)}, u32[]{:S(2)}) %collective-permute-start) | collective-permute-done | bytes 524320 | tf_op jit(solution)/shard_map/ppermute | solution.py:29
  16.3 5.5 %collective-permute-start.2 = (bf16[4,256,256]{2,1,0:T(8,128)(2,1)S(1)}, bf16[4,256,256]{2,1,0:T(8,128)(2,1)S(1)}, u32[]{:S(2)}, u32[]{:S(2)}) collective-permute-start(bf16[4,256,256]{2,1,0:T(8,128)(2,1)S(1)} %collective-permute-done.rows.rows2), channel_id=1, source_target_pairs={{0,2},{1,3},{2,4},{3,5},{4,6},{5,7},{6,8},{7,9},{8,10},{9,11},{10,... | collective-permute-start | bytes 1572872 | tf_op jit(solution)/shard_map/ppermute | solution.py:29
  21.8 0.9 %pack.1.packed = bf16[1,272,256]{2,1,0:T(8,128)(2,1)S(1)} custom-call(bf16[1,256,256]{2,1,0:T(8,128)(2,1)} %col_desc.1, bf16[1,2,256]{2,1,0:T(2,128)(2,1)} %coords.1), custom_call_target="tpu_custom_call" | custom-call | tf_op jit(solution)/shard_map/pack/pallas_call | solution.py:176
  22.7 4.3 %collective-permute-start.3 = (bf16[1,272,256]{2,1,0:T(8,128)(2,1)S(1)}, bf16[1,272,256]{2,1,0:T(8,128)(2,1)S(1)}, u32[]{:S(2)}, u32[]{:S(2)}) collective-permute-start(bf16[1,272,256]{2,1,0:T(8,128)(2,1)S(1)} %pack.1.packed), channel_id=1, source_target_pairs={{0,64},{1,65},{2,66},{3,67},{4,68},{5,69},{6,70},{7,71},{8,72},{9,... | collective-permute-start | bytes 417800 | tf_op jit(solution)/shard_map/ppermute | solution.py:29
  27.0 4.9 %collective-permute-start.1 = (bf16[1,272,256]{2,1,0:T(8,128)(2,1)S(1)}, bf16[1,272,256]{2,1,0:T(8,128)(2,1)S(1)}, u32[]{:S(2)}, u32[]{:S(2)}) collective-permute-start(bf16[1,272,256]{2,1,0:T(8,128)(2,1)S(1)} %pack.1.packed), channel_id=1, source_target_pairs={{0,32},{1,33},{2,34},{3,35},{4,36},{5,37},{6,38},{7,39},{8,40},{9,... | collective-permute-start | bytes 417800 | tf_op jit(solution)/shard_map/ppermute | solution.py:29
  32.0 4.8 %collective-permute-done.3.packed.image4 = bf16[1,272,256]{2,1,0:T(8,128)(2,1)S(1)} collective-permute-done((bf16[1,272,256]{2,1,0:T(8,128)(2,1)S(1)}, bf16[1,272,256]{2,1,0:T(8,128)(2,1)S(1)}, u32[]{:S(2)}, u32[]{:S(2)}) %collective-permute-start.3) | collective-permute-done | bytes 139296 | tf_op jit(solution)/shard_map/ppermute | solution.py:29
  36.7 5.4 %collective-permute-done.1.packed.image2 = bf16[1,272,256]{2,1,0:T(8,128)(2,1)S(1)} collective-permute-done((bf16[1,272,256]{2,1,0:T(8,128)(2,1)S(1)}, bf16[1,272,256]{2,1,0:T(8,128)(2,1)S(1)}, u32[]{:S(2)}, u32[]{:S(2)}) %collective-permute-start.1) | collective-permute-done | bytes 139296 | tf_op jit(solution)/shard_map/ppermute | solution.py:29
  42.1 1.9 %collective-permute-start.5 = (bf16[2,272,256]{2,1,0:T(8,128)(2,1)S(1)}, bf16[2,272,256]{2,1,0:T(8,128)(2,1)S(1)}, u32[]{:S(2)}, u32[]{:S(2)}) collective-permute-start(bf16[2,272,256]{2,1,0:T(8,128)(2,1)S(1)} %join.1), channel_id=1, source_target_pairs={{0,31},{1,16},{2,17},{3,18},{4,19},{5,20},{6,21},{7,22},{8,23},{9,... | collective-permute-start | bytes 835592 | tf_op jit(solution)/shard_map/ppermute | solution.py:29
  44.1 1.9 %collective-permute-start.4 = (bf16[1,272,256]{2,1,0:T(8,128)(2,1)S(1)}, bf16[1,272,256]{2,1,0:T(8,128)(2,1)S(1)}, u32[]{:S(2)}, u32[]{:S(2)}) collective-permute-start(bf16[1,272,256]{2,1,0:T(8,128)(2,1)S(1)} %pack.1.packed), channel_id=1, source_target_pairs={{0,31},{1,16},{2,17},{3,18},{4,19},{5,20},{6,21},{7,22},{8,23},{9,... | collective-permute-start | bytes 417800 | tf_op jit(solution)/shard_map/ppermute | solution.py:29
  46.0 0.0 copy-done
  46.0 1.2 %first.1 = (f32[3,4,256]{2,1,0:T(4,128)S(1)}, s32[40,256]{1,0:T(8,128)S(1)}) custom-call(s32[2048]{0:T(1024)} %row_counts.1, s32[512]{0:T(512)} %col_counts.1, s32[2048]{0:T(1024)} %row_cluster.1, s32[512]{0:T(512)} %col_cluster.1, bf16[4,256,256]{2,1,0:T(8,128)(2,1)S(1)} %copy-done, bf16[1,272,256]{2,1,0:T(8,128)(2,1)S(1)} %pack.1.packed), custom_call_target="tpu_custom_call" | custom-call | tf_op jit(solution)/shard_map/first/pallas_call | solution.py:201
  47.2 8.9 %collective-permute-done.4.direct = bf16[1,272,256]{2,1,0:T(8,128)(2,1)S(1)} collective-permute-done((bf16[1,272,256]{2,1,0:T(8,128)(2,1)S(1)}, bf16[1,272,256]{2,1,0:T(8,128)(2,1)S(1)}, u32[]{:S(2)}, u32[]{:S(2)}) %collective-permute-start.4) | collective-permute-done | bytes 139296 | tf_op jit(solution)/shard_map/ppermute | solution.py:29
  56.1 0.0 collective-permute-done.5.images
  56.1 0.0 collective-permute-done.2.rows.rows4
  56.1 3.1 %odd.1 = f32[3,3,4,256]{3,2,1,0:T(4,128)S(1)} custom-call(s32[40,256]{1,0:T(8,128)S(1)} %get-tuple-element.8.meta, bf16[4,256,256]{2,1,0:T(8,128)(2,1)S(1)} %copy-done, bf16[4,256,256]{2,1,0:T(8,128)(2,1)S(1)} %collective-permute-done.rows.rows2, bf16[4,256,256]{2,1,0:T(8,128)(2,1)S(1)} %collective-permute-done.2.rows.rows4, ...), custom_call_target="tpu_custom_call" | custom-call | tf_op jit(solution)/shard_map/odd/pallas_call | solution.py:215
  59.2 2.0 %collective-permute-start.6 = (f32[3,3,4,256]{3,2,1,0:T(4,128)S(1)}, f32[3,3,4,256]{3,2,1,0:T(4,128)S(1)}, u32[]{:S(2)}, u32[]{:S(2)}) collective-permute-start(f32[3,3,4,256]{3,2,1,0:T(4,128)S(1)} %odd.1), channel_id=1, source_target_pairs={{0,1},{1,2},{2,3},{3,4},{4,5},{5,6},{6,7},{7,8},{8,9},{9,10},{10,1... | collective-permute-start | bytes 110600 | tf_op jit(solution)/shard_map/ppermute | solution.py:29
  61.2 0.7 %second.1.res2 = f32[3,4,256]{2,1,0:T(4,128)S(1)} custom-call(s32[40,256]{1,0:T(8,128)S(1)} %get-tuple-element.8.meta, bf16[4,256,256]{2,1,0:T(8,128)(2,1)S(1)} %collective-permute-done.rows.rows2, bf16[1,272,256]{2,1,0:T(8,128)(2,1)S(1)} %collective-permute-done.1.packed.image2), custom_call_target="tpu_custom_call" | custom-call | tf_op jit(solution)/shard_map/second/pallas_call | solution.py:208
  61.9 1.2 %fourth.1.res4 = f32[3,4,256]{2,1,0:T(4,128)S(1)} custom-call(s32[40,256]{1,0:T(8,128)S(1)} %get-tuple-element.8.meta, bf16[4,256,256]{2,1,0:T(8,128)(2,1)S(1)} %collective-permute-done.2.rows.rows4, bf16[1,272,256]{2,1,0:T(8,128)(2,1)S(1)} %collective-permute-done.3.packed.image4), custom_call_target="tpu_custom_call" | custom-call | tf_op jit(solution)/shard_map/fourth/pallas_call | solution.py:223
  63.1 2.8 %collective-permute-done.6.home = f32[3,3,4,256]{3,2,1,0:T(4,128)S(1)} collective-permute-done((f32[3,3,4,256]{3,2,1,0:T(4,128)S(1)}, f32[3,3,4,256]{3,2,1,0:T(4,128)S(1)}, u32[]{:S(2)}, u32[]{:S(2)}) %collective-permute-start.6) | collective-permute-done | bytes 36896 | tf_op jit(solution)/shard_map/ppermute | solution.py:29
  66.0 0.7 %final.1 = f32[6,3,4,256]{3,2,1,0:T(4,128)} custom-call(f32[3,4,256]{2,1,0:T(4,128)S(1)} %get-tuple-element.7.res0, f32[3,4,256]{2,1,0:T(4,128)S(1)} %second.1.res2, f32[3,4,256]{2,1,0:T(4,128)S(1)} %fourth.1.res4, f32[3,3,4,256]{3,2,1,0:T(4,128)S(1)} %collective-permute-done.6.home), custom_call_target="tpu_custom_call" | custom-call | tf_op jit(solution)/shard_map/final/pallas_call | solution.py:230
  (1 shorter events, 0.0 us)
Async XLA Ops:
  0.0 46.0 %copy-start = (bf16[4,256,256]{2,1,0:T(8,128)(2,1)S(1)}, bf16[4,256,256]{2,1,0:T(8,128)(2,1)}, u32[]{:S(2)}) copy-start(bf16[4,256,256]{2,1,0:T(8,128)(2,1)} %rows0.1) | copy-start | bytes 1572868
  0.0 16.3 %collective-permute-start = (bf16[4,256,256]{2,1,0:T(8,128)(2,1)}, bf16[4,256,256]{2,1,0:T(8,128)(2,1)S(1)}, u32[]{:S(2)}, u32[]{:S(2)}) collective-permute-start(bf16[4,256,256]{2,1,0:T(8,128)(2,1)} %rows0.1), channel_id=1, source_target_pairs={{0,2},{1,3},{2,4},{3,5},{4,6},{5,7},{6,8},{7,9},{8,10},{9,11},{10,... | collective-permute-start | bytes 1572872 | tf_op jit(solution)/shard_map/ppermute | solution.py:29
  16.3 39.8 %collective-permute-start.2 = (bf16[4,256,256]{2,1,0:T(8,128)(2,1)S(1)}, bf16[4,256,256]{2,1,0:T(8,128)(2,1)S(1)}, u32[]{:S(2)}, u32[]{:S(2)}) collective-permute-start(bf16[4,256,256]{2,1,0:T(8,128)(2,1)S(1)} %collective-permute-done.rows.rows2), channel_id=1, source_target_pairs={{0,2},{1,3},{2,4},{3,5},{4,6},{5,7},{6,8},{7,9},{8,10},{9,11},{10,... | collective-permute-start | bytes 1572872 | tf_op jit(solution)/shard_map/ppermute | solution.py:29
  22.7 14.0 %collective-permute-start.3 = (bf16[1,272,256]{2,1,0:T(8,128)(2,1)S(1)}, bf16[1,272,256]{2,1,0:T(8,128)(2,1)S(1)}, u32[]{:S(2)}, u32[]{:S(2)}) collective-permute-start(bf16[1,272,256]{2,1,0:T(8,128)(2,1)S(1)} %pack.1.packed), channel_id=1, source_target_pairs={{0,64},{1,65},{2,66},{3,67},{4,68},{5,69},{6,70},{7,71},{8,72},{9,... | collective-permute-start | bytes 417800 | tf_op jit(solution)/shard_map/ppermute | solution.py:29
  27.0 15.1 %collective-permute-start.1 = (bf16[1,272,256]{2,1,0:T(8,128)(2,1)S(1)}, bf16[1,272,256]{2,1,0:T(8,128)(2,1)S(1)}, u32[]{:S(2)}, u32[]{:S(2)}) collective-permute-start(bf16[1,272,256]{2,1,0:T(8,128)(2,1)S(1)} %pack.1.packed), channel_id=1, source_target_pairs={{0,32},{1,33},{2,34},{3,35},{4,36},{5,37},{6,38},{7,39},{8,40},{9,... | collective-permute-start | bytes 417800 | tf_op jit(solution)/shard_map/ppermute | solution.py:29
  42.1 14.0 %collective-permute-start.5 = (bf16[2,272,256]{2,1,0:T(8,128)(2,1)S(1)}, bf16[2,272,256]{2,1,0:T(8,128)(2,1)S(1)}, u32[]{:S(2)}, u32[]{:S(2)}) collective-permute-start(bf16[2,272,256]{2,1,0:T(8,128)(2,1)S(1)} %join.1), channel_id=1, source_target_pairs={{0,31},{1,16},{2,17},{3,18},{4,19},{5,20},{6,21},{7,22},{8,23},{9,... | collective-permute-start | bytes 835592 | tf_op jit(solution)/shard_map/ppermute | solution.py:29
  44.1 12.0 %collective-permute-start.4 = (bf16[1,272,256]{2,1,0:T(8,128)(2,1)S(1)}, bf16[1,272,256]{2,1,0:T(8,128)(2,1)S(1)}, u32[]{:S(2)}, u32[]{:S(2)}) collective-permute-start(bf16[1,272,256]{2,1,0:T(8,128)(2,1)S(1)} %pack.1.packed), channel_id=1, source_target_pairs={{0,31},{1,16},{2,17},{3,18},{4,19},{5,20},{6,21},{7,22},{8,23},{9,... | collective-permute-start | bytes 417800 | tf_op jit(solution)/shard_map/ppermute | solution.py:29
  59.2 6.7 %collective-permute-start.6 = (f32[3,3,4,256]{3,2,1,0:T(4,128)S(1)}, f32[3,3,4,256]{3,2,1,0:T(4,128)S(1)}, u32[]{:S(2)}, u32[]{:S(2)}) collective-permute-start(f32[3,3,4,256]{3,2,1,0:T(4,128)S(1)} %odd.1), channel_id=1, source_target_pairs={{0,1},{1,2},{2,3},{3,4},{4,5},{5,6},{6,7},{7,8},{8,9},{9,10},{10,1... | collective-permute-start | bytes 110600 | tf_op jit(solution)/shard_map/ppermute | solution.py:29

commit v2 on v1

--- a/solution.py
+++ b/solution.py
@@ -123,23 +123,39 @@
     panel(0, rows, packed.at[0], meta, out)
 
 
-def second_kernel(meta, rows, packed, out):
-    panel(2, rows, packed.at[0], meta, out)
-
-
-def odd_kernel(meta, rows0, rows2, rows4, direct, images, out):
-    even_row = lax.rem(lax.axis_index("row"), 2) == 0
-
-    @pl.when(even_row)
+def even_row():
+    return lax.rem(lax.axis_index("row"), 2) == 0
+
+
+def early_kernel(meta, rows0, rows2, image2, direct, res2, out):
+    panel(2, rows2, image2.at[0], meta, res2)
+
+    @pl.when(jnp.logical_not(even_row()))
+    def _():
+        panel(1, rows0, direct.at[0], meta, out.at[0])
+
+
+def middle_kernel(meta, rows0, rows2, images, kept, out):
+    del kept
+    even = even_row()
+
+    @pl.when(even)
     def _():
         panel(1, rows0, images.at[0], meta, out.at[0])
-        panel(3, rows2, images.at[1], meta, out.at[1])
+
+    panel(3, rows2, images.at[even.astype(jnp.int32)], meta, out.at[1])
+
+
+def late_kernel(meta, rows4, direct, images, kept, out):
+    del kept
+    even = even_row()
+
+    @pl.when(even)
+    def _():
         panel(5, rows4, direct.at[0], meta, out.at[2])
 
-    @pl.when(jnp.logical_not(even_row))
-    def _():
-        panel(1, rows0, direct.at[0], meta, out.at[0])
-        panel(3, rows2, images.at[0], meta, out.at[1])
+    @pl.when(jnp.logical_not(even))
+    def _():
         panel(5, rows4, images.at[1], meta, out.at[2])
 
 
@@ -205,20 +221,32 @@
         out_specs=(VMEM, VMEM),
         name="first",
     )(row_counts, col_counts, row_cluster, col_cluster, rows0, near(packed))
-    res2 = pl.pallas_call(
-        second_kernel,
-        out_shape=many(),
-        in_specs=[VMEM] * 3,
-        out_specs=VMEM,
-        name="second",
-    )(near(meta), near(rows2), near(image2))
+    meta = near(meta)
+    rows2, rows4, image2 = near(rows2), near(rows4), near(image2)
+    direct, images = near(direct), near(images)
+    res2, res135 = pl.pallas_call(
+        early_kernel,
+        out_shape=(many(), many(3)),
+        in_specs=[VMEM] * 5,
+        out_specs=(VMEM, VMEM),
+        name="early",
+    )(meta, rows0, rows2, image2, direct)
     res135 = pl.pallas_call(
-        odd_kernel,
+        middle_kernel,
         out_shape=many(3),
-        in_specs=[VMEM] * 6,
-        out_specs=VMEM,
-        name="odd",
-    )(near(meta), rows0, near(rows2), near(rows4), near(direct), near(images))
+        in_specs=[VMEM] * 5,
+        out_specs=VMEM,
+        input_output_aliases={4: 0},
+        name="middle",
+    )(meta, rows0, rows2, images, near(res135))
+    res135 = pl.pallas_call(
+        late_kernel,
+        out_shape=many(3),
+        in_specs=[VMEM] * 5,
+        out_specs=VMEM,
+        input_output_aliases={4: 0},
+        name="late",
+    )(meta, rows4, direct, images, near(res135))
     home = shift(res135, 0, 1)
     res4 = pl.pallas_call(
         fourth_kernel,
@@ -226,7 +254,7 @@
         in_specs=[VMEM] * 3,
         out_specs=VMEM,
         name="fourth",
-    )(near(meta), near(rows4), near(image4))
+    )(meta, rows4, near(image4))
     done = pl.pallas_call(
         final_kernel,
         out_shape=jax.ShapeDtypeStruct((STEPS, 3, ri, slots), jnp.float32),

time: 67 us -> 67.7 us (1.010)
  waiting for transfers between devices: 33.4 us -> 34.1 us
    ppermute x7, waiting for transfers between devices: 33.4 us -> 34.1 us  [move(): return lax.ppermute(value, ('row', 'col'), perm)]
    pallas_call x2 -> x3, Pallas kernels: 3.82 us -> 3.83 us  [the longest x1 1.91 us: local(): pl.pallas_call(middle_kernel, out_shape=many(3), in_specs=[VMEM] * 5, out...]
  transfers between devices with their start and end apart: 7 -> 7, of which waited for: 5 -> 5; matrix products, arithmetic and copies ran while one was open for 0% -> 0% of each run, Pallas kernels for 6% -> 9%
where the time goes in v2:
time: 67.7 us; the launch traced here: 67.4 us
  waiting for transfers between devices  34.1 us (50%)
  starting transfers between devices  25.3 us (37%)
  Pallas kernels  7.84 us (12%)
    ppermute x7, waiting for transfers between devices, move(): return lax.ppermute(value, ('row', 'col'), perm)  34.1 us
    ppermute x7, starting transfers between devices, move(): return lax.ppermute(value, ('row', 'col'), perm)  25.3 us
    pallas_call x1, Pallas kernels, local(): pl.pallas_call(middle_kernel, out_shape=many(3), in_specs=[VMEM] * 5, out...  1.91 us
  transfers between devices with their start and end apart: 7, of which 5 were waited for; matrix products, arithmetic and copies ran while one was open for 0% of the time, Pallas kernels for 9%

profile of v2, /device:TPU:24, one launch (start us, length us, event | category | flops | bytes accessed | tf_op | source)
XLA Modules:
  0.0 67.4 jit_solution(10017854391819865981)
XLA Ops:
  0.0 0.0 copy-start
  0.0 4.8 %collective-permute-start = (bf16[4,256,256]{2,1,0:T(8,128)(2,1)}, bf16[4,256,256]{2,1,0:T(8,128)(2,1)S(1)}, u32[]{:S(2)}, u32[]{:S(2)}) collective-permute-start(bf16[4,256,256]{2,1,0:T(8,128)(2,1)} %rows0.3), channel_id=1, source_target_pairs={{0,2},{1,3},{2,4},{3,5},{4,6},{5,7},{6,8},{7,9},{8,10},{9,11},{10,... | collective-permute-start | bytes 1572872 | tf_op jit(solution)/shard_map/ppermute | solution.py:29
  4.8 11.5 %collective-permute-done.rows2 = bf16[4,256,256]{2,1,0:T(8,128)(2,1)S(1)} collective-permute-done((bf16[4,256,256]{2,1,0:T(8,128)(2,1)}, bf16[4,256,256]{2,1,0:T(8,128)(2,1)S(1)}, u32[]{:S(2)}, u32[]{:S(2)}) %collective-permute-start) | collective-permute-done | bytes 524320 | tf_op jit(solution)/shard_map/ppermute | solution.py:29
  16.3 5.5 %collective-permute-start.3 = (bf16[4,256,256]{2,1,0:T(8,128)(2,1)S(1)}, bf16[4,256,256]{2,1,0:T(8,128)(2,1)S(1)}, u32[]{:S(2)}, u32[]{:S(2)}) collective-permute-start(bf16[4,256,256]{2,1,0:T(8,128)(2,1)S(1)} %collective-permute-done.rows2), channel_id=1, source_target_pairs={{0,2},{1,3},{2,4},{3,5},{4,6},{5,7},{6,8},{7,9},{8,10},{9,11},{10,... | collective-permute-start | bytes 1572872 | tf_op jit(solution)/shard_map/ppermute | solution.py:29
  21.8 0.9 %pack.1.packed = bf16[1,272,256]{2,1,0:T(8,128)(2,1)S(1)} custom-call(bf16[1,256,256]{2,1,0:T(8,128)(2,1)} %col_desc.1, bf16[1,2,256]{2,1,0:T(2,128)(2,1)} %coords.1), custom_call_target="tpu_custom_call" | custom-call | tf_op jit(solution)/shard_map/pack/pallas_call | solution.py:192
  22.7 4.3 %collective-permute-start.4 = (bf16[1,272,256]{2,1,0:T(8,128)(2,1)S(1)}, bf16[1,272,256]{2,1,0:T(8,128)(2,1)S(1)}, u32[]{:S(2)}, u32[]{:S(2)}) collective-permute-start(bf16[1,272,256]{2,1,0:T(8,128)(2,1)S(1)} %pack.1.packed), channel_id=1, source_target_pairs={{0,64},{1,65},{2,66},{3,67},{4,68},{5,69},{6,70},{7,71},{8,72},{9,... | collective-permute-start | bytes 417800 | tf_op jit(solution)/shard_map/ppermute | solution.py:29
  27.0 4.9 %collective-permute-start.1 = (bf16[1,272,256]{2,1,0:T(8,128)(2,1)S(1)}, bf16[1,272,256]{2,1,0:T(8,128)(2,1)S(1)}, u32[]{:S(2)}, u32[]{:S(2)}) collective-permute-start(bf16[1,272,256]{2,1,0:T(8,128)(2,1)S(1)} %pack.1.packed), channel_id=1, source_target_pairs={{0,32},{1,33},{2,34},{3,35},{4,36},{5,37},{6,38},{7,39},{8,40},{9,... | collective-permute-start | bytes 417800 | tf_op jit(solution)/shard_map/ppermute | solution.py:29
  32.0 4.8 %collective-permute-done.4.packed.image4 = bf16[1,272,256]{2,1,0:T(8,128)(2,1)S(1)} collective-permute-done((bf16[1,272,256]{2,1,0:T(8,128)(2,1)S(1)}, bf16[1,272,256]{2,1,0:T(8,128)(2,1)S(1)}, u32[]{:S(2)}, u32[]{:S(2)}) %collective-permute-start.4) | collective-permute-done | bytes 139296 | tf_op jit(solution)/shard_map/ppermute | solution.py:29
  36.7 5.4 %collective-permute-done.1.image2 = bf16[1,272,256]{2,1,0:T(8,128)(2,1)S(1)} collective-permute-done((bf16[1,272,256]{2,1,0:T(8,128)(2,1)S(1)}, bf16[1,272,256]{2,1,0:T(8,128)(2,1)S(1)}, u32[]{:S(2)}, u32[]{:S(2)}) %collective-permute-start.1) | collective-permute-done | bytes 139296 | tf_op jit(solution)/shard_map/ppermute | solution.py:29
  42.1 1.9 %collective-permute-start.5 = (bf16[2,272,256]{2,1,0:T(8,128)(2,1)S(1)}, bf16[2,272,256]{2,1,0:T(8,128)(2,1)S(1)}, u32[]{:S(2)}, u32[]{:S(2)}) collective-permute-start(bf16[2,272,256]{2,1,0:T(8,128)(2,1)S(1)} %join.1), channel_id=1, source_target_pairs={{0,31},{1,16},{2,17},{3,18},{4,19},{5,20},{6,21},{7,22},{8,23},{9,... | collective-permute-start | bytes 835592 | tf_op jit(solution)/shard_map/ppermute | solution.py:29
  44.1 1.9 %collective-permute-start.2 = (bf16[1,272,256]{2,1,0:T(8,128)(2,1)S(1)}, bf16[1,272,256]{2,1,0:T(8,128)(2,1)S(1)}, u32[]{:S(2)}, u32[]{:S(2)}) collective-permute-start(bf16[1,272,256]{2,1,0:T(8,128)(2,1)S(1)} %pack.1.packed), channel_id=1, source_target_pairs={{0,31},{1,16},{2,17},{3,18},{4,19},{5,20},{6,21},{7,22},{8,23},{9,... | collective-permute-start | bytes 417800 | tf_op jit(solution)/shard_map/ppermute | solution.py:29
  46.0 0.0 copy-done
  46.0 1.2 %first.1 = (f32[3,4,256]{2,1,0:T(4,128)S(1)}, s32[40,256]{1,0:T(8,128)S(1)}) custom-call(s32[2048]{0:T(1024)} %row_counts.1, s32[512]{0:T(512)} %col_counts.1, s32[2048]{0:T(1024)} %row_cluster.1, s32[512]{0:T(512)} %col_cluster.1, bf16[4,256,256]{2,1,0:T(8,128)(2,1)S(1)} %copy-done, bf16[1,272,256]{2,1,0:T(8,128)(2,1)S(1)} %pack.1.packed), custom_call_target="tpu_custom_call" | custom-call | tf_op jit(solution)/shard_map/first/pallas_call | solution.py:217
  47.2 8.9 %collective-permute-done.2.direct = bf16[1,272,256]{2,1,0:T(8,128)(2,1)S(1)} collective-permute-done((bf16[1,272,256]{2,1,0:T(8,128)(2,1)S(1)}, bf16[1,272,256]{2,1,0:T(8,128)(2,1)S(1)}, u32[]{:S(2)}, u32[]{:S(2)}) %collective-permute-start.2) | collective-permute-done | bytes 139296 | tf_op jit(solution)/shard_map/ppermute | solution.py:29
  56.1 0.7 %early.1 = (f32[3,4,256]{2,1,0:T(4,128)S(1)}, f32[3,3,4,256]{3,2,1,0:T(4,128)S(1)}) custom-call(s32[40,256]{1,0:T(8,128)S(1)} %get-tuple-element.10.meta, bf16[4,256,256]{2,1,0:T(8,128)(2,1)S(1)} %copy-done, bf16[4,256,256]{2,1,0:T(8,128)(2,1)S(1)} %collective-permute-done.rows2, bf16[1,272,256]{2,1,0:T(8,128)(2,1)S(1)} %collective-permute-done.1.image2, ...), custom_call_target="tpu_custom_call" | custom-call | tf_op jit(solution)/shard_map/early/pallas_call | solution.py:227
  56.8 0.0 collective-permute-done.5.images
  56.8 1.9 %middle.1.kept = f32[3,3,4,256]{3,2,1,0:T(4,128)S(1)} custom-call(s32[40,256]{1,0:T(8,128)S(1)} %get-tuple-element.10.meta, bf16[4,256,256]{2,1,0:T(8,128)(2,1)S(1)} %copy-done, bf16[4,256,256]{2,1,0:T(8,128)(2,1)S(1)} %collective-permute-done.rows2, bf16[2,272,256]{2,1,0:T(8,128)(2,1)S(1)} %collective-permute-done.5.images, ...), custom_call_target="tpu_custom_call", output_to_operand_aliasing={{}: (4, {})} | custom-call | tf_op jit(solution)/shard_map/middle/pallas_call | solution.py:234
  58.7 0.0 collective-permute-done.3.rows.rows4
  58.7 1.2 %late.1 = f32[3,3,4,256]{3,2,1,0:T(4,128)S(1)} custom-call(s32[40,256]{1,0:T(8,128)S(1)} %get-tuple-element.10.meta, bf16[4,256,256]{2,1,0:T(8,128)(2,1)S(1)} %collective-permute-done.3.rows.rows4, bf16[1,272,256]{2,1,0:T(8,128)(2,1)S(1)} %collective-permute-done.2.direct, ...), custom_call_target="tpu_custom_call", output_to_operand_aliasing={{}: (4, {})} | custom-call | tf_op jit(solution)/shard_map/late/pallas_call | solution.py:242
  59.9 2.0 %collective-permute-start.6 = (f32[3,3,4,256]{3,2,1,0:T(4,128)S(1)}, f32[3,3,4,256]{3,2,1,0:T(4,128)S(1)}, u32[]{:S(2)}, u32[]{:S(2)}) collective-permute-start(f32[3,3,4,256]{3,2,1,0:T(4,128)S(1)} %late.1), channel_id=1, source_target_pairs={{0,1},{1,2},{2,3},{3,4},{4,5},{5,6},{6,7},{7,8},{8,9},{9,10},{10,1... | collective-permute-start | bytes 110600 | tf_op jit(solution)/shard_map/ppermute | solution.py:29
  61.9 1.2 %fourth.1.res4 = f32[3,4,256]{2,1,0:T(4,128)S(1)} custom-call(s32[40,256]{1,0:T(8,128)S(1)} %get-tuple-element.10.meta, bf16[4,256,256]{2,1,0:T(8,128)(2,1)S(1)} %collective-permute-done.3.rows.rows4, bf16[1,272,256]{2,1,0:T(8,128)(2,1)S(1)} %collective-permute-done.4.packed.image4), custom_call_target="tpu_custom_call" | custom-call | tf_op jit(solution)/shard_map/fourth/pallas_call | solution.py:251
  63.2 3.5 %collective-permute-done.6.home = f32[3,3,4,256]{3,2,1,0:T(4,128)S(1)} collective-permute-done((f32[3,3,4,256]{3,2,1,0:T(4,128)S(1)}, f32[3,3,4,256]{3,2,1,0:T(4,128)S(1)}, u32[]{:S(2)}, u32[]{:S(2)}) %collective-permute-start.6) | collective-permute-done | bytes 36896 | tf_op jit(solution)/shard_map/ppermute | solution.py:29
  66.7 0.7 final.1
  (1 shorter events, 0.0 us)
Async XLA Ops:
  0.0 46.0 %copy-start = (bf16[4,256,256]{2,1,0:T(8,128)(2,1)S(1)}, bf16[4,256,256]{2,1,0:T(8,128)(2,1)}, u32[]{:S(2)}) copy-start(bf16[4,256,256]{2,1,0:T(8,128)(2,1)} %rows0.3) | copy-start | bytes 1572868
  0.0 16.3 %collective-permute-start = (bf16[4,256,256]{2,1,0:T(8,128)(2,1)}, bf16[4,256,256]{2,1,0:T(8,128)(2,1)S(1)}, u32[]{:S(2)}, u32[]{:S(2)}) collective-permute-start(bf16[4,256,256]{2,1,0:T(8,128)(2,1)} %rows0.3), channel_id=1, source_target_pairs={{0,2},{1,3},{2,4},{3,5},{4,6},{5,7},{6,8},{7,9},{8,10},{9,11},{10,... | collective-permute-start | bytes 1572872 | tf_op jit(solution)/shard_map/ppermute | solution.py:29
  16.3 42.4 %collective-permute-start.3 = (bf16[4,256,256]{2,1,0:T(8,128)(2,1)S(1)}, bf16[4,256,256]{2,1,0:T(8,128)(2,1)S(1)}, u32[]{:S(2)}, u32[]{:S(2)}) collective-permute-start(bf16[4,256,256]{2,1,0:T(8,128)(2,1)S(1)} %collective-permute-done.rows2), channel_id=1, source_target_pairs={{0,2},{1,3},{2,4},{3,5},{4,6},{5,7},{6,8},{7,9},{8,10},{9,11},{10,... | collective-permute-start | bytes 1572872 | tf_op jit(solution)/shard_map/ppermute | solution.py:29
  22.7 14.0 %collective-permute-start.4 = (bf16[1,272,256]{2,1,0:T(8,128)(2,1)S(1)}, bf16[1,272,256]{2,1,0:T(8,128)(2,1)S(1)}, u32[]{:S(2)}, u32[]{:S(2)}) collective-permute-start(bf16[1,272,256]{2,1,0:T(8,128)(2,1)S(1)} %pack.1.packed), channel_id=1, source_target_pairs={{0,64},{1,65},{2,66},{3,67},{4,68},{5,69},{6,70},{7,71},{8,72},{9,... | collective-permute-start | bytes 417800 | tf_op jit(solution)/shard_map/ppermute | solution.py:29
  27.0 15.1 %collective-permute-start.1 = (bf16[1,272,256]{2,1,0:T(8,128)(2,1)S(1)}, bf16[1,272,256]{2,1,0:T(8,128)(2,1)S(1)}, u32[]{:S(2)}, u32[]{:S(2)}) collective-permute-start(bf16[1,272,256]{2,1,0:T(8,128)(2,1)S(1)} %pack.1.packed), channel_id=1, source_target_pairs={{0,32},{1,33},{2,34},{3,35},{4,36},{5,37},{6,38},{7,39},{8,40},{9,... | collective-permute-start | bytes 417800 | tf_op jit(solution)/shard_map/ppermute | solution.py:29
  42.1 14.7 %collective-permute-start.5 = (bf16[2,272,256]{2,1,0:T(8,128)(2,1)S(1)}, bf16[2,272,256]{2,1,0:T(8,128)(2,1)S(1)}, u32[]{:S(2)}, u32[]{:S(2)}) collective-permute-start(bf16[2,272,256]{2,1,0:T(8,128)(2,1)S(1)} %join.1), channel_id=1, source_target_pairs={{0,31},{1,16},{2,17},{3,18},{4,19},{5,20},{6,21},{7,22},{8,23},{9,... | collective-permute-start | bytes 835592 | tf_op jit(solution)/shard_map/ppermute | solution.py:29
  44.1 12.0 %collective-permute-start.2 = (bf16[1,272,256]{2,1,0:T(8,128)(2,1)S(1)}, bf16[1,272,256]{2,1,0:T(8,128)(2,1)S(1)}, u32[]{:S(2)}, u32[]{:S(2)}) collective-permute-start(bf16[1,272,256]{2,1,0:T(8,128)(2,1)S(1)} %pack.1.packed), channel_id=1, source_target_pairs={{0,31},{1,16},{2,17},{3,18},{4,19},{5,20},{6,21},{7,22},{8,23},{9,... | collective-permute-start | bytes 417800 | tf_op jit(solution)/shard_map/ppermute | solution.py:29
  59.9 6.7 %collective-permute-start.6 = (f32[3,3,4,256]{3,2,1,0:T(4,128)S(1)}, f32[3,3,4,256]{3,2,1,0:T(4,128)S(1)}, u32[]{:S(2)}, u32[]{:S(2)}) collective-permute-start(f32[3,3,4,256]{3,2,1,0:T(4,128)S(1)} %late.1), channel_id=1, source_target_pairs={{0,1},{1,2},{2,3},{3,4},{4,5},{5,6},{6,7},{7,8},{8,9},{9,10},{10,1... | collective-permute-start | bytes 110600 | tf_op jit(solution)/shard_map/ppermute | solution.py:29

commit v3 on v2

--- a/solution.py
+++ b/solution.py
@@ -9,7 +9,8 @@
 
 
 STEPS = 6
-TABLE = 16
+TABLE = 8
+PARTS = 4
 COLS = 24
 FLAGS = 32
 inv_temp = 10.0
@@ -78,9 +79,14 @@
 
 def pack_kernel(col_desc, coords, packed, table_in, sems):
     k = col_desc.shape[1]
-    copies = [
-        pltpu.make_async_copy(coords, table_in, sems.at[0]),
-        pltpu.make_async_copy(col_desc, packed.at[:, :k], sems.at[1]),
+    part = k // PARTS
+    copies = [pltpu.make_async_copy(coords, table_in, sems.at[0])] + [
+        pltpu.make_async_copy(
+            col_desc.at[:, n * part : (n + 1) * part],
+            packed.at[:, n * part : (n + 1) * part],
+            sems.at[n + 1],
+        )
+        for n in range(PARTS)
     ]
     for copy in copies:
         copy.start()
@@ -92,7 +98,8 @@
     table = jnp.where(at == 0, 1.0, jnp.where(at == 1, x, jnp.where(at == 2, y, zero)))
     table = table.astype(jnp.bfloat16)
     packed[0, k:] = table
-    copies[1].wait()
+    for copy in copies[1:]:
+        copy.wait()
 
 
 def join_kernel(image2, image4, out):
@@ -196,7 +203,7 @@
         out_specs=VMEM,
         scratch_shapes=[
             pltpu.VMEM(col_coords.shape, jnp.bfloat16),
-            pltpu.SemaphoreType.DMA((2,)),
+            pltpu.SemaphoreType.DMA((PARTS + 1,)),
         ],
         name="pack",
     )(col_desc, col_coords)

time: 67.7 us -> 67.5 us (level)
  no operation moved by 1% of the time
where the time goes in v3:
time: 67.5 us; the launch traced here: 67.1 us
  waiting for transfers between devices  33.9 us (50%)
  starting transfers between devices  25.3 us (37%)
  Pallas kernels  7.76 us (11%)
    ppermute x7, waiting for transfers between devices, move(): return lax.ppermute(value, ('row', 'col'), perm)  33.9 us
    ppermute x7, starting transfers between devices, move(): return lax.ppermute(value, ('row', 'col'), perm)  25.3 us
    pallas_call x1, Pallas kernels, local(): pl.pallas_call(middle_kernel, out_shape=many(3), in_specs=[VMEM] * 5, out...  1.91 us
  transfers between devices with their start and end apart: 7, of which 5 were waited for; matrix products, arithmetic and copies ran while one was open for 0% of the time, Pallas kernels for 9%

profile of v3, /device:TPU:24, one launch (start us, length us, event | category | flops | bytes accessed | tf_op | source)
XLA Modules:
  0.0 67.1 jit_solution(14391219900218548191)
XLA Ops:
  0.0 0.0 copy-start
  0.0 4.8 %collective-permute-start = (bf16[4,256,256]{2,1,0:T(8,128)(2,1)}, bf16[4,256,256]{2,1,0:T(8,128)(2,1)S(1)}, u32[]{:S(2)}, u32[]{:S(2)}) collective-permute-start(bf16[4,256,256]{2,1,0:T(8,128)(2,1)} %rows0.3), channel_id=1, source_target_pairs={{0,2},{1,3},{2,4},{3,5},{4,6},{5,7},{6,8},{7,9},{8,10},{9,11},{10,... | collective-permute-start | bytes 1572872 | tf_op jit(solution)/shard_map/ppermute | solution.py:30
  4.8 11.5 %collective-permute-done.rows2 = bf16[4,256,256]{2,1,0:T(8,128)(2,1)S(1)} collective-permute-done((bf16[4,256,256]{2,1,0:T(8,128)(2,1)}, bf16[4,256,256]{2,1,0:T(8,128)(2,1)S(1)}, u32[]{:S(2)}, u32[]{:S(2)}) %collective-permute-start) | collective-permute-done | bytes 524320 | tf_op jit(solution)/shard_map/ppermute | solution.py:30
  16.3 5.5 %collective-permute-start.3 = (bf16[4,256,256]{2,1,0:T(8,128)(2,1)S(1)}, bf16[4,256,256]{2,1,0:T(8,128)(2,1)S(1)}, u32[]{:S(2)}, u32[]{:S(2)}) collective-permute-start(bf16[4,256,256]{2,1,0:T(8,128)(2,1)S(1)} %collective-permute-done.rows2), channel_id=1, source_target_pairs={{0,2},{1,3},{2,4},{3,5},{4,6},{5,7},{6,8},{7,9},{8,10},{9,11},{10,... | collective-permute-start | bytes 1572872 | tf_op jit(solution)/shard_map/ppermute | solution.py:30
  21.8 0.9 %pack.1.packed = bf16[1,264,256]{2,1,0:T(8,128)(2,1)S(1)} custom-call(bf16[1,256,256]{2,1,0:T(8,128)(2,1)} %col_desc.1, bf16[1,2,256]{2,1,0:T(2,128)(2,1)} %coords.1), custom_call_target="tpu_custom_call" | custom-call | tf_op jit(solution)/shard_map/pack/pallas_call | solution.py:199
  22.7 4.3 %collective-permute-start.4 = (bf16[1,264,256]{2,1,0:T(8,128)(2,1)S(1)}, bf16[1,264,256]{2,1,0:T(8,128)(2,1)S(1)}, u32[]{:S(2)}, u32[]{:S(2)}) collective-permute-start(bf16[1,264,256]{2,1,0:T(8,128)(2,1)S(1)} %pack.1.packed), channel_id=1, source_target_pairs={{0,64},{1,65},{2,66},{3,67},{4,68},{5,69},{6,70},{7,71},{8,72},{9,... | collective-permute-start | bytes 405512 | tf_op jit(solution)/shard_map/ppermute | solution.py:30
  27.0 4.9 %collective-permute-start.1 = (bf16[1,264,256]{2,1,0:T(8,128)(2,1)S(1)}, bf16[1,264,256]{2,1,0:T(8,128)(2,1)S(1)}, u32[]{:S(2)}, u32[]{:S(2)}) collective-permute-start(bf16[1,264,256]{2,1,0:T(8,128)(2,1)S(1)} %pack.1.packed), channel_id=1, source_target_pairs={{0,32},{1,33},{2,34},{3,35},{4,36},{5,37},{6,38},{7,39},{8,40},{9,... | collective-permute-start | bytes 405512 | tf_op jit(solution)/shard_map/ppermute | solution.py:30
  31.9 4.7 %collective-permute-done.4.packed.image4 = bf16[1,264,256]{2,1,0:T(8,128)(2,1)S(1)} collective-permute-done((bf16[1,264,256]{2,1,0:T(8,128)(2,1)S(1)}, bf16[1,264,256]{2,1,0:T(8,128)(2,1)S(1)}, u32[]{:S(2)}, u32[]{:S(2)}) %collective-permute-start.4) | collective-permute-done | bytes 135200 | tf_op jit(solution)/shard_map/ppermute | solution.py:30
  36.6 5.3 %collective-permute-done.1.image2 = bf16[1,264,256]{2,1,0:T(8,128)(2,1)S(1)} collective-permute-done((bf16[1,264,256]{2,1,0:T(8,128)(2,1)S(1)}, bf16[1,264,256]{2,1,0:T(8,128)(2,1)S(1)}, u32[]{:S(2)}, u32[]{:S(2)}) %collective-permute-start.1) | collective-permute-done | bytes 135200 | tf_op jit(solution)/shard_map/ppermute | solution.py:30
  41.9 1.9 %collective-permute-start.5 = (bf16[2,264,256]{2,1,0:T(8,128)(2,1)S(1)}, bf16[2,264,256]{2,1,0:T(8,128)(2,1)S(1)}, u32[]{:S(2)}, u32[]{:S(2)}) collective-permute-start(bf16[2,264,256]{2,1,0:T(8,128)(2,1)S(1)} %join.1), channel_id=1, source_target_pairs={{0,31},{1,16},{2,17},{3,18},{4,19},{5,20},{6,21},{7,22},{8,23},{9,... | collective-permute-start | bytes 811016 | tf_op jit(solution)/shard_map/ppermute | solution.py:30
  43.8 1.9 %collective-permute-start.2 = (bf16[1,264,256]{2,1,0:T(8,128)(2,1)S(1)}, bf16[1,264,256]{2,1,0:T(8,128)(2,1)S(1)}, u32[]{:S(2)}, u32[]{:S(2)}) collective-permute-start(bf16[1,264,256]{2,1,0:T(8,128)(2,1)S(1)} %pack.1.packed), channel_id=1, source_target_pairs={{0,31},{1,16},{2,17},{3,18},{4,19},{5,20},{6,21},{7,22},{8,23},{9,... | collective-permute-start | bytes 405512 | tf_op jit(solution)/shard_map/ppermute | solution.py:30
  45.8 0.0 copy-done
  45.8 1.2 %first.1 = (f32[3,4,256]{2,1,0:T(4,128)S(1)}, s32[40,256]{1,0:T(8,128)S(1)}) custom-call(s32[2048]{0:T(1024)} %row_counts.1, s32[512]{0:T(512)} %col_counts.1, s32[2048]{0:T(1024)} %row_cluster.1, s32[512]{0:T(512)} %col_cluster.1, bf16[4,256,256]{2,1,0:T(8,128)(2,1)S(1)} %copy-done, bf16[1,264,256]{2,1,0:T(8,128)(2,1)S(1)} %pack.1.packed), custom_call_target="tpu_custom_call" | custom-call | tf_op jit(solution)/shard_map/first/pallas_call | solution.py:224
  47.0 8.9 %collective-permute-done.2.direct = bf16[1,264,256]{2,1,0:T(8,128)(2,1)S(1)} collective-permute-done((bf16[1,264,256]{2,1,0:T(8,128)(2,1)S(1)}, bf16[1,264,256]{2,1,0:T(8,128)(2,1)S(1)}, u32[]{:S(2)}, u32[]{:S(2)}) %collective-permute-start.2) | collective-permute-done | bytes 135200 | tf_op jit(solution)/shard_map/ppermute | solution.py:30
  55.8 0.7 %early.1 = (f32[3,4,256]{2,1,0:T(4,128)S(1)}, f32[3,3,4,256]{3,2,1,0:T(4,128)S(1)}) custom-call(s32[40,256]{1,0:T(8,128)S(1)} %get-tuple-element.10.meta, bf16[4,256,256]{2,1,0:T(8,128)(2,1)S(1)} %copy-done, bf16[4,256,256]{2,1,0:T(8,128)(2,1)S(1)} %collective-permute-done.rows2, bf16[1,264,256]{2,1,0:T(8,128)(2,1)S(1)} %collective-permute-done.1.image2, ...), custom_call_target="tpu_custom_call" | custom-call | tf_op jit(solution)/shard_map/early/pallas_call | solution.py:234
  56.5 0.0 collective-permute-done.5.images
  56.5 1.9 %middle.1.kept = f32[3,3,4,256]{3,2,1,0:T(4,128)S(1)} custom-call(s32[40,256]{1,0:T(8,128)S(1)} %get-tuple-element.10.meta, bf16[4,256,256]{2,1,0:T(8,128)(2,1)S(1)} %copy-done, bf16[4,256,256]{2,1,0:T(8,128)(2,1)S(1)} %collective-permute-done.rows2, bf16[2,264,256]{2,1,0:T(8,128)(2,1)S(1)} %collective-permute-done.5.images, ...), custom_call_target="tpu_custom_call", output_to_operand_aliasing={{}: (4, {})} | custom-call | tf_op jit(solution)/shard_map/middle/pallas_call | solution.py:241
  58.4 0.0 collective-permute-done.3.rows.rows4
  58.4 1.2 %late.1 = f32[3,3,4,256]{3,2,1,0:T(4,128)S(1)} custom-call(s32[40,256]{1,0:T(8,128)S(1)} %get-tuple-element.10.meta, bf16[4,256,256]{2,1,0:T(8,128)(2,1)S(1)} %collective-permute-done.3.rows.rows4, bf16[1,264,256]{2,1,0:T(8,128)(2,1)S(1)} %collective-permute-done.2.direct, ...), custom_call_target="tpu_custom_call", output_to_operand_aliasing={{}: (4, {})} | custom-call | tf_op jit(solution)/shard_map/late/pallas_call | solution.py:249
  59.6 1.9 %collective-permute-start.6 = (f32[3,3,4,256]{3,2,1,0:T(4,128)S(1)}, f32[3,3,4,256]{3,2,1,0:T(4,128)S(1)}, u32[]{:S(2)}, u32[]{:S(2)}) collective-permute-start(f32[3,3,4,256]{3,2,1,0:T(4,128)S(1)} %late.1), channel_id=1, source_target_pairs={{0,1},{1,2},{2,3},{3,4},{4,5},{5,6},{6,7},{7,8},{8,9},{9,10},{10,1... | collective-permute-start | bytes 110600 | tf_op jit(solution)/shard_map/ppermute | solution.py:30
  61.6 1.2 %fourth.1.res4 = f32[3,4,256]{2,1,0:T(4,128)S(1)} custom-call(s32[40,256]{1,0:T(8,128)S(1)} %get-tuple-element.10.meta, bf16[4,256,256]{2,1,0:T(8,128)(2,1)S(1)} %collective-permute-done.3.rows.rows4, bf16[1,264,256]{2,1,0:T(8,128)(2,1)S(1)} %collective-permute-done.4.packed.image4), custom_call_target="tpu_custom_call" | custom-call | tf_op jit(solution)/shard_map/fourth/pallas_call | solution.py:258
  62.8 3.6 %collective-permute-done.6.home = f32[3,3,4,256]{3,2,1,0:T(4,128)S(1)} collective-permute-done((f32[3,3,4,256]{3,2,1,0:T(4,128)S(1)}, f32[3,3,4,256]{3,2,1,0:T(4,128)S(1)}, u32[]{:S(2)}, u32[]{:S(2)}) %collective-permute-start.6) | collective-permute-done | bytes 36896 | tf_op jit(solution)/shard_map/ppermute | solution.py:30
  66.4 0.7 final.1
  (1 shorter events, 0.0 us)
Async XLA Ops:
  0.0 45.8 %copy-start = (bf16[4,256,256]{2,1,0:T(8,128)(2,1)S(1)}, bf16[4,256,256]{2,1,0:T(8,128)(2,1)}, u32[]{:S(2)}) copy-start(bf16[4,256,256]{2,1,0:T(8,128)(2,1)} %rows0.3) | copy-start | bytes 1572868
  0.0 16.3 %collective-permute-start = (bf16[4,256,256]{2,1,0:T(8,128)(2,1)}, bf16[4,256,256]{2,1,0:T(8,128)(2,1)S(1)}, u32[]{:S(2)}, u32[]{:S(2)}) collective-permute-start(bf16[4,256,256]{2,1,0:T(8,128)(2,1)} %rows0.3), channel_id=1, source_target_pairs={{0,2},{1,3},{2,4},{3,5},{4,6},{5,7},{6,8},{7,9},{8,10},{9,11},{10,... | collective-permute-start | bytes 1572872 | tf_op jit(solution)/shard_map/ppermute | solution.py:30
  16.3 42.1 %collective-permute-start.3 = (bf16[4,256,256]{2,1,0:T(8,128)(2,1)S(1)}, bf16[4,256,256]{2,1,0:T(8,128)(2,1)S(1)}, u32[]{:S(2)}, u32[]{:S(2)}) collective-permute-start(bf16[4,256,256]{2,1,0:T(8,128)(2,1)S(1)} %collective-permute-done.rows2), channel_id=1, source_target_pairs={{0,2},{1,3},{2,4},{3,5},{4,6},{5,7},{6,8},{7,9},{8,10},{9,11},{10,... | collective-permute-start | bytes 1572872 | tf_op jit(solution)/shard_map/ppermute | solution.py:30
  22.7 13.9 %collective-permute-start.4 = (bf16[1,264,256]{2,1,0:T(8,128)(2,1)S(1)}, bf16[1,264,256]{2,1,0:T(8,128)(2,1)S(1)}, u32[]{:S(2)}, u32[]{:S(2)}) collective-permute-start(bf16[1,264,256]{2,1,0:T(8,128)(2,1)S(1)} %pack.1.packed), channel_id=1, source_target_pairs={{0,64},{1,65},{2,66},{3,67},{4,68},{5,69},{6,70},{7,71},{8,72},{9,... | collective-permute-start | bytes 405512 | tf_op jit(solution)/shard_map/ppermute | solution.py:30
  27.0 14.9 %collective-permute-start.1 = (bf16[1,264,256]{2,1,0:T(8,128)(2,1)S(1)}, bf16[1,264,256]{2,1,0:T(8,128)(2,1)S(1)}, u32[]{:S(2)}, u32[]{:S(2)}) collective-permute-start(bf16[1,264,256]{2,1,0:T(8,128)(2,1)S(1)} %pack.1.packed), channel_id=1, source_target_pairs={{0,32},{1,33},{2,34},{3,35},{4,36},{5,37},{6,38},{7,39},{8,40},{9,... | collective-permute-start | bytes 405512 | tf_op jit(solution)/shard_map/ppermute | solution.py:30
  41.9 14.6 %collective-permute-start.5 = (bf16[2,264,256]{2,1,0:T(8,128)(2,1)S(1)}, bf16[2,264,256]{2,1,0:T(8,128)(2,1)S(1)}, u32[]{:S(2)}, u32[]{:S(2)}) collective-permute-start(bf16[2,264,256]{2,1,0:T(8,128)(2,1)S(1)} %join.1), channel_id=1, source_target_pairs={{0,31},{1,16},{2,17},{3,18},{4,19},{5,20},{6,21},{7,22},{8,23},{9,... | collective-permute-start | bytes 811016 | tf_op jit(solution)/shard_map/ppermute | solution.py:30
  43.8 12.0 %collective-permute-start.2 = (bf16[1,264,256]{2,1,0:T(8,128)(2,1)S(1)}, bf16[1,264,256]{2,1,0:T(8,128)(2,1)S(1)}, u32[]{:S(2)}, u32[]{:S(2)}) collective-permute-start(bf16[1,264,256]{2,1,0:T(8,128)(2,1)S(1)} %pack.1.packed), channel_id=1, source_target_pairs={{0,31},{1,16},{2,17},{3,18},{4,19},{5,20},{6,21},{7,22},{8,23},{9,... | collective-permute-start | bytes 405512 | tf_op jit(solution)/shard_map/ppermute | solution.py:30
  59.6 6.7 %collective-permute-start.6 = (f32[3,3,4,256]{3,2,1,0:T(4,128)S(1)}, f32[3,3,4,256]{3,2,1,0:T(4,128)S(1)}, u32[]{:S(2)}, u32[]{:S(2)}) collective-permute-start(f32[3,3,4,256]{3,2,1,0:T(4,128)S(1)} %late.1), channel_id=1, source_target_pairs={{0,1},{1,2},{2,3},{3,4},{4,5},{5,6},{6,7},{7,8},{8,9},{9,10},{10,1... | collective-permute-start | bytes 110600 | tf_op jit(solution)/shard_map/ppermute | solution.py:30

commit v4 on v3

--- a/solution.py
+++ b/solution.py
@@ -166,21 +166,25 @@
         panel(5, rows4, images.at[1], meta, out.at[2])
 
 
-def fourth_kernel(meta, rows, packed, out):
-    panel(4, rows, packed.at[0], meta, out)
-
-
-def final_kernel(res0, res2, res4, home, out, sems):
+def write_all(parts, out, sems):
     copies = [
-        pltpu.make_async_copy(home.at[n], out.at[2 * n + 1], sems.at[n]) for n in range(3)
-    ] + [
-        pltpu.make_async_copy(res, out.at[2 * n], sems.at[3 + n])
-        for n, res in enumerate((res0, res2, res4))
+        pltpu.make_async_copy(part, out.at[at], sems.at[n])
+        for n, (part, at) in enumerate(parts)
     ]
     for copy in copies:
         copy.start()
     for copy in copies:
         copy.wait()
+
+
+def fourth_kernel(meta, rows, packed, res0, res2, out, res4, sems):
+    panel(4, rows, packed.at[0], meta, res4)
+    write_all(((res0, 0), (res2, 2), (res4, 4)), out, sems)
+
+
+def final_kernel(home, kept, out, sems):
+    del kept
+    write_all([(home.at[n], 2 * n + 1) for n in range(3)], out, sems)
 
 
 def near(value):
@@ -255,21 +259,28 @@
         name="late",
     )(meta, rows4, direct, images, near(res135))
     home = shift(res135, 0, 1)
-    res4 = pl.pallas_call(
+    whole = jax.ShapeDtypeStruct((STEPS, 3, ri, slots), jnp.float32)
+    far = pl.BlockSpec(memory_space=pl.ANY)
+    evens = pl.pallas_call(
         fourth_kernel,
-        out_shape=many(),
-        in_specs=[VMEM] * 3,
-        out_specs=VMEM,
+        out_shape=whole,
+        in_specs=[VMEM] * 5,
+        out_specs=far,
+        scratch_shapes=[
+            pltpu.VMEM((3, ri, slots), jnp.float32),
+            pltpu.SemaphoreType.DMA((3,)),
+        ],
         name="fourth",
-    )(meta, rows4, near(image4))
+    )(meta, rows4, near(image4), near(res0), near(res2))
     done = pl.pallas_call(
         final_kernel,
-        out_shape=jax.ShapeDtypeStruct((STEPS, 3, ri, slots), jnp.float32),
-        in_specs=[VMEM] * 4,
-        out_specs=pl.BlockSpec(memory_space=pl.ANY),
-        scratch_shapes=[pltpu.SemaphoreType.DMA((6,))],
+        out_shape=whole,
+        in_specs=[VMEM, far],
+        out_specs=far,
+        scratch_shapes=[pltpu.SemaphoreType.DMA((3,))],
+        input_output_aliases={1: 0},
         name="final",
-    )(near(res0), near(res2), near(res4), near(home))
+    )(near(home), evens)
     return jnp.transpose(done, (0, 2, 1, 3))
 
 

time: 67.5 us -> 67.4 us (level)
  transfers between devices with their start and end apart: 7 -> 7, of which waited for: 5 -> 5; matrix products, arithmetic and copies ran while one was open for 0% -> 0% of each run, Pallas kernels for 9% -> 10%
where the time goes in v4:
time: 67.4 us; the launch traced here: 67 us
  waiting for transfers between devices  33.3 us (49%)
  starting transfers between devices  25.3 us (38%)
  Pallas kernels  8.36 us (12%)
    ppermute x7, waiting for transfers between devices, move(): return lax.ppermute(value, ('row', 'col'), perm)  33.3 us
    ppermute x7, starting transfers between devices, move(): return lax.ppermute(value, ('row', 'col'), perm)  25.3 us
    pallas_call x1, Pallas kernels, local(): pl.pallas_call(middle_kernel, out_shape=many(3), in_specs=[VMEM] * 5, out...  1.91 us
    pallas_call x1, Pallas kernels, local(): pl.pallas_call(fourth_kernel, out_shape=whole, in_specs=[VMEM] * 5, out_s...  1.86 us
  transfers between devices with their start and end apart: 7, of which 5 were waited for; matrix products, arithmetic and copies ran while one was open for 0% of the time, Pallas kernels for 10%

profile of v4, /device:TPU:24, one launch (start us, length us, event | category | flops | bytes accessed | tf_op | source)
XLA Modules:
  0.0 67.0 jit_solution(10431489175882086945)
XLA Ops:
  0.0 0.0 copy-start
  0.0 4.8 %collective-permute-start = (bf16[4,256,256]{2,1,0:T(8,128)(2,1)}, bf16[4,256,256]{2,1,0:T(8,128)(2,1)S(1)}, u32[]{:S(2)}, u32[]{:S(2)}) collective-permute-start(bf16[4,256,256]{2,1,0:T(8,128)(2,1)} %rows0.3), channel_id=1, source_target_pairs={{0,2},{1,3},{2,4},{3,5},{4,6},{5,7},{6,8},{7,9},{8,10},{9,11},{10,... | collective-permute-start | bytes 1572872 | tf_op jit(solution)/shard_map/ppermute | solution.py:30
  4.8 11.5 %collective-permute-done.rows2 = bf16[4,256,256]{2,1,0:T(8,128)(2,1)S(1)} collective-permute-done((bf16[4,256,256]{2,1,0:T(8,128)(2,1)}, bf16[4,256,256]{2,1,0:T(8,128)(2,1)S(1)}, u32[]{:S(2)}, u32[]{:S(2)}) %collective-permute-start) | collective-permute-done | bytes 524320 | tf_op jit(solution)/shard_map/ppermute | solution.py:30
  16.3 5.5 %collective-permute-start.1 = (bf16[4,256,256]{2,1,0:T(8,128)(2,1)S(1)}, bf16[4,256,256]{2,1,0:T(8,128)(2,1)S(1)}, u32[]{:S(2)}, u32[]{:S(2)}) collective-permute-start(bf16[4,256,256]{2,1,0:T(8,128)(2,1)S(1)} %collective-permute-done.rows2), channel_id=1, source_target_pairs={{0,2},{1,3},{2,4},{3,5},{4,6},{5,7},{6,8},{7,9},{8,10},{9,11},{10,... | collective-permute-start | bytes 1572872 | tf_op jit(solution)/shard_map/ppermute | solution.py:30
  21.8 0.9 %pack.1.packed = bf16[1,264,256]{2,1,0:T(8,128)(2,1)S(1)} custom-call(bf16[1,256,256]{2,1,0:T(8,128)(2,1)} %col_desc.1, bf16[1,2,256]{2,1,0:T(2,128)(2,1)} %coords.1), custom_call_target="tpu_custom_call" | custom-call | tf_op jit(solution)/shard_map/pack/pallas_call | solution.py:203
  22.7 4.3 %collective-permute-start.4 = (bf16[1,264,256]{2,1,0:T(8,128)(2,1)S(1)}, bf16[1,264,256]{2,1,0:T(8,128)(2,1)S(1)}, u32[]{:S(2)}, u32[]{:S(2)}) collective-permute-start(bf16[1,264,256]{2,1,0:T(8,128)(2,1)S(1)} %pack.1.packed), channel_id=1, source_target_pairs={{0,64},{1,65},{2,66},{3,67},{4,68},{5,69},{6,70},{7,71},{8,72},{9,... | collective-permute-start | bytes 405512 | tf_op jit(solution)/shard_map/ppermute | solution.py:30
  27.0 4.9 %collective-permute-start.3 = (bf16[1,264,256]{2,1,0:T(8,128)(2,1)S(1)}, bf16[1,264,256]{2,1,0:T(8,128)(2,1)S(1)}, u32[]{:S(2)}, u32[]{:S(2)}) collective-permute-start(bf16[1,264,256]{2,1,0:T(8,128)(2,1)S(1)} %pack.1.packed), channel_id=1, source_target_pairs={{0,32},{1,33},{2,34},{3,35},{4,36},{5,37},{6,38},{7,39},{8,40},{9,... | collective-permute-start | bytes 405512 | tf_op jit(solution)/shard_map/ppermute | solution.py:30
  31.9 4.7 %collective-permute-done.4.image4.packed = bf16[1,264,256]{2,1,0:T(8,128)(2,1)S(1)} collective-permute-done((bf16[1,264,256]{2,1,0:T(8,128)(2,1)S(1)}, bf16[1,264,256]{2,1,0:T(8,128)(2,1)S(1)}, u32[]{:S(2)}, u32[]{:S(2)}) %collective-permute-start.4) | collective-permute-done | bytes 135200 | tf_op jit(solution)/shard_map/ppermute | solution.py:30
  36.6 5.3 %collective-permute-done.3.image2 = bf16[1,264,256]{2,1,0:T(8,128)(2,1)S(1)} collective-permute-done((bf16[1,264,256]{2,1,0:T(8,128)(2,1)S(1)}, bf16[1,264,256]{2,1,0:T(8,128)(2,1)S(1)}, u32[]{:S(2)}, u32[]{:S(2)}) %collective-permute-start.3) | collective-permute-done | bytes 135200 | tf_op jit(solution)/shard_map/ppermute | solution.py:30
  41.9 1.9 %collective-permute-start.5 = (bf16[2,264,256]{2,1,0:T(8,128)(2,1)S(1)}, bf16[2,264,256]{2,1,0:T(8,128)(2,1)S(1)}, u32[]{:S(2)}, u32[]{:S(2)}) collective-permute-start(bf16[2,264,256]{2,1,0:T(8,128)(2,1)S(1)} %join.1), channel_id=1, source_target_pairs={{0,31},{1,16},{2,17},{3,18},{4,19},{5,20},{6,21},{7,22},{8,23},{9,... | collective-permute-start | bytes 811016 | tf_op jit(solution)/shard_map/ppermute | solution.py:30
  43.8 1.9 %collective-permute-start.2 = (bf16[1,264,256]{2,1,0:T(8,128)(2,1)S(1)}, bf16[1,264,256]{2,1,0:T(8,128)(2,1)S(1)}, u32[]{:S(2)}, u32[]{:S(2)}) collective-permute-start(bf16[1,264,256]{2,1,0:T(8,128)(2,1)S(1)} %pack.1.packed), channel_id=1, source_target_pairs={{0,31},{1,16},{2,17},{3,18},{4,19},{5,20},{6,21},{7,22},{8,23},{9,... | collective-permute-start | bytes 405512 | tf_op jit(solution)/shard_map/ppermute | solution.py:30
  45.8 0.0 copy-done
  45.8 1.2 %first.1 = (f32[3,4,256]{2,1,0:T(4,128)S(1)}, s32[40,256]{1,0:T(8,128)S(1)}) custom-call(s32[2048]{0:T(1024)} %row_counts.1, s32[512]{0:T(512)} %col_counts.1, s32[2048]{0:T(1024)} %row_cluster.1, s32[512]{0:T(512)} %col_cluster.1, bf16[4,256,256]{2,1,0:T(8,128)(2,1)S(1)} %copy-done, bf16[1,264,256]{2,1,0:T(8,128)(2,1)S(1)} %pack.1.packed), custom_call_target="tpu_custom_call" | custom-call | tf_op jit(solution)/shard_map/first/pallas_call | solution.py:228
  47.0 8.9 %collective-permute-done.2.direct = bf16[1,264,256]{2,1,0:T(8,128)(2,1)S(1)} collective-permute-done((bf16[1,264,256]{2,1,0:T(8,128)(2,1)S(1)}, bf16[1,264,256]{2,1,0:T(8,128)(2,1)S(1)}, u32[]{:S(2)}, u32[]{:S(2)}) %collective-permute-start.2) | collective-permute-done | bytes 135200 | tf_op jit(solution)/shard_map/ppermute | solution.py:30
  55.8 0.7 %early.1 = (f32[3,4,256]{2,1,0:T(4,128)S(1)}, f32[3,3,4,256]{3,2,1,0:T(4,128)S(1)}) custom-call(s32[40,256]{1,0:T(8,128)S(1)} %get-tuple-element.9.meta, bf16[4,256,256]{2,1,0:T(8,128)(2,1)S(1)} %copy-done, bf16[4,256,256]{2,1,0:T(8,128)(2,1)S(1)} %collective-permute-done.rows2, bf16[1,264,256]{2,1,0:T(8,128)(2,1)S(1)} %collective-permute-done.3.image2, ...), custom_call_target="tpu_custom_call" | custom-call | tf_op jit(solution)/shard_map/early/pallas_call | solution.py:238
  56.5 0.0 collective-permute-done.5.images
  56.5 1.9 %middle.1.kept = f32[3,3,4,256]{3,2,1,0:T(4,128)S(1)} custom-call(s32[40,256]{1,0:T(8,128)S(1)} %get-tuple-element.9.meta, bf16[4,256,256]{2,1,0:T(8,128)(2,1)S(1)} %copy-done, bf16[4,256,256]{2,1,0:T(8,128)(2,1)S(1)} %collective-permute-done.rows2, bf16[2,264,256]{2,1,0:T(8,128)(2,1)S(1)} %collective-permute-done.5.images, ...), custom_call_target="tpu_custom_call", output_to_operand_aliasing={{}: (4, {})} | custom-call | tf_op jit(solution)/shard_map/middle/pallas_call | solution.py:245
  58.4 0.0 collective-permute-done.1.rows4.rows
  58.4 1.2 %late.1 = f32[3,3,4,256]{3,2,1,0:T(4,128)S(1)} custom-call(s32[40,256]{1,0:T(8,128)S(1)} %get-tuple-element.9.meta, bf16[4,256,256]{2,1,0:T(8,128)(2,1)S(1)} %collective-permute-done.1.rows4.rows, bf16[1,264,256]{2,1,0:T(8,128)(2,1)S(1)} %collective-permute-done.2.direct, ...), custom_call_target="tpu_custom_call", output_to_operand_aliasing={{}: (4, {})} | custom-call | tf_op jit(solution)/shard_map/late/pallas_call | solution.py:253
  59.6 1.9 %collective-permute-start.6 = (f32[3,3,4,256]{3,2,1,0:T(4,128)S(1)}, f32[3,3,4,256]{3,2,1,0:T(4,128)S(1)}, u32[]{:S(2)}, u32[]{:S(2)}) collective-permute-start(f32[3,3,4,256]{3,2,1,0:T(4,128)S(1)} %late.1), channel_id=1, source_target_pairs={{0,1},{1,2},{2,3},{3,4},{4,5},{5,6},{6,7},{7,8},{8,9},{9,10},{10,1... | collective-permute-start | bytes 110600 | tf_op jit(solution)/shard_map/ppermute | solution.py:30
  61.6 1.9 %fourth.1.kept = f32[6,3,4,256]{3,2,1,0:T(4,128)} custom-call(s32[40,256]{1,0:T(8,128)S(1)} %get-tuple-element.9.meta, bf16[4,256,256]{2,1,0:T(8,128)(2,1)S(1)} %collective-permute-done.1.rows4.rows, bf16[1,264,256]{2,1,0:T(8,128)(2,1)S(1)} %collective-permute-done.4.image4.packed, f32[3,4,256]{2,1,0:T(4,128)S(1)} %get-tuple-element.11.res0, ...), custom_call_target="tpu_custom_call" | custom-call | tf_op jit(solution)/shard_map/fourth/pallas_call | solution.py:264
  63.4 3.0 %collective-permute-done.6.home = f32[3,3,4,256]{3,2,1,0:T(4,128)S(1)} collective-permute-done((f32[3,3,4,256]{3,2,1,0:T(4,128)S(1)}, f32[3,3,4,256]{3,2,1,0:T(4,128)S(1)}, u32[]{:S(2)}, u32[]{:S(2)}) %collective-permute-start.6) | collective-permute-done | bytes 36896 | tf_op jit(solution)/shard_map/ppermute | solution.py:30
  66.4 0.6 final.1
  (1 shorter events, 0.0 us)
Async XLA Ops:
  0.0 45.8 %copy-start = (bf16[4,256,256]{2,1,0:T(8,128)(2,1)S(1)}, bf16[4,256,256]{2,1,0:T(8,128)(2,1)}, u32[]{:S(2)}) copy-start(bf16[4,256,256]{2,1,0:T(8,128)(2,1)} %rows0.3) | copy-start | bytes 1572868
  0.0 16.3 %collective-permute-start = (bf16[4,256,256]{2,1,0:T(8,128)(2,1)}, bf16[4,256,256]{2,1,0:T(8,128)(2,1)S(1)}, u32[]{:S(2)}, u32[]{:S(2)}) collective-permute-start(bf16[4,256,256]{2,1,0:T(8,128)(2,1)} %rows0.3), channel_id=1, source_target_pairs={{0,2},{1,3},{2,4},{3,5},{4,6},{5,7},{6,8},{7,9},{8,10},{9,11},{10,... | collective-permute-start | bytes 1572872 | tf_op jit(solution)/shard_map/ppermute | solution.py:30
  16.3 42.1 %collective-permute-start.1 = (bf16[4,256,256]{2,1,0:T(8,128)(2,1)S(1)}, bf16[4,256,256]{2,1,0:T(8,128)(2,1)S(1)}, u32[]{:S(2)}, u32[]{:S(2)}) collective-permute-start(bf16[4,256,256]{2,1,0:T(8,128)(2,1)S(1)} %collective-permute-done.rows2), channel_id=1, source_target_pairs={{0,2},{1,3},{2,4},{3,5},{4,6},{5,7},{6,8},{7,9},{8,10},{9,11},{10,... | collective-permute-start | bytes 1572872 | tf_op jit(solution)/shard_map/ppermute | solution.py:30
  22.7 13.9 %collective-permute-start.4 = (bf16[1,264,256]{2,1,0:T(8,128)(2,1)S(1)}, bf16[1,264,256]{2,1,0:T(8,128)(2,1)S(1)}, u32[]{:S(2)}, u32[]{:S(2)}) collective-permute-start(bf16[1,264,256]{2,1,0:T(8,128)(2,1)S(1)} %pack.1.packed), channel_id=1, source_target_pairs={{0,64},{1,65},{2,66},{3,67},{4,68},{5,69},{6,70},{7,71},{8,72},{9,... | collective-permute-start | bytes 405512 | tf_op jit(solution)/shard_map/ppermute | solution.py:30
  27.0 14.9 %collective-permute-start.3 = (bf16[1,264,256]{2,1,0:T(8,128)(2,1)S(1)}, bf16[1,264,256]{2,1,0:T(8,128)(2,1)S(1)}, u32[]{:S(2)}, u32[]{:S(2)}) collective-permute-start(bf16[1,264,256]{2,1,0:T(8,128)(2,1)S(1)} %pack.1.packed), channel_id=1, source_target_pairs={{0,32},{1,33},{2,34},{3,35},{4,36},{5,37},{6,38},{7,39},{8,40},{9,... | collective-permute-start | bytes 405512 | tf_op jit(solution)/shard_map/ppermute | solution.py:30
  41.9 14.6 %collective-permute-start.5 = (bf16[2,264,256]{2,1,0:T(8,128)(2,1)S(1)}, bf16[2,264,256]{2,1,0:T(8,128)(2,1)S(1)}, u32[]{:S(2)}, u32[]{:S(2)}) collective-permute-start(bf16[2,264,256]{2,1,0:T(8,128)(2,1)S(1)} %join.1), channel_id=1, source_target_pairs={{0,31},{1,16},{2,17},{3,18},{4,19},{5,20},{6,21},{7,22},{8,23},{9,... | collective-permute-start | bytes 811016 | tf_op jit(solution)/shard_map/ppermute | solution.py:30
  43.8 12.0 %collective-permute-start.2 = (bf16[1,264,256]{2,1,0:T(8,128)(2,1)S(1)}, bf16[1,264,256]{2,1,0:T(8,128)(2,1)S(1)}, u32[]{:S(2)}, u32[]{:S(2)}) collective-permute-start(bf16[1,264,256]{2,1,0:T(8,128)(2,1)S(1)} %pack.1.packed), channel_id=1, source_target_pairs={{0,31},{1,16},{2,17},{3,18},{4,19},{5,20},{6,21},{7,22},{8,23},{9,... | collective-permute-start | bytes 405512 | tf_op jit(solution)/shard_map/ppermute | solution.py:30
  59.6 6.7 %collective-permute-start.6 = (f32[3,3,4,256]{3,2,1,0:T(4,128)S(1)}, f32[3,3,4,256]{3,2,1,0:T(4,128)S(1)}, u32[]{:S(2)}, u32[]{:S(2)}) collective-permute-start(f32[3,3,4,256]{3,2,1,0:T(4,128)S(1)} %late.1), channel_id=1, source_target_pairs={{0,1},{1,2},{2,3},{3,4},{4,5},{5,6},{6,7},{7,8},{8,9},{9,10},{10,1... | collective-permute-start | bytes 110600 | tf_op jit(solution)/shard_map/ppermute | solution.py:30

commit v5 on v4

--- a/solution.py
+++ b/solution.py
@@ -34,10 +34,9 @@
     return move(value, lambda i: i + by_row, by_col)
 
 
-def one_pair(rows, packed, row_count, col_count):
-    k = packed.shape[0] - TABLE
+def one_pair(rows, image, table, row_count, col_count):
     scores = inv_temp * lax.dot_general(
-        packed[:k], rows, (((1,), (1,)), ((), ())), preferred_element_type=jnp.float32
+        image, rows, (((1,), (1,)), ((), ())), preferred_element_type=jnp.float32
     )
     col_ok = lax.broadcasted_iota(jnp.int32, scores.shape, 0) < col_count
     row_ok = lax.broadcasted_iota(jnp.int32, (1, scores.shape[1]), 1) < row_count
@@ -49,7 +48,7 @@
     col_inv = 1.0 / jnp.sum(col_exp, axis=1, keepdims=True)
     prob = ((row_exp * row_inv) * (col_exp * col_inv)).astype(jnp.bfloat16)
     return lax.dot_general(
-        packed[k:], prob, (((1,), (0,)), ((), ())), preferred_element_type=jnp.float32
+        table, prob, (((1,), (0,)), ((), ())), preferred_element_type=jnp.float32
     )
 
 
@@ -58,21 +57,34 @@
     out_ref[...] = jnp.zeros_like(out_ref)
     flags = jnp.max(meta_ref[pl.ds(FLAGS + step, 1), :].astype(jnp.float32)).astype(jnp.int32)
 
+    slots = rows_ref.shape[1]
+    half = slots // 2
+    few_cols = (flags >> (2 * ri)) & 1
+
     def body(r, carry):
-        @pl.when(((flags >> r) & 1) == 1)
-        def _():
+        kind = ((flags >> r) & 1) * (1 + 2 * few_cols + ((flags >> (ri + r)) & 1))
+
+        def pair(q, k):
             found = one_pair(
-                rows_ref[r],
-                packed_ref[...],
-                meta_ref[pl.ds(step * ri + r, 1), :],
-                meta_ref[pl.ds(COLS + step, 1), :],
+                rows_ref[r, :q],
+                packed_ref[:k],
+                packed_ref[slots:, :k],
+                meta_ref[pl.ds(step * ri + r, 1), :][:, :q],
+                meta_ref[pl.ds(COLS + step, 1), :][:, :q],
             )
+            if q < slots:
+                rest = jnp.zeros((found.shape[0], slots - q), jnp.float32)
+                found = jnp.concatenate([found, rest], axis=1)
             for c in range(3):
                 out_ref[c, pl.ds(r, 1), :] = found[c : c + 1]
 
+        for n, (q, k) in enumerate(
+            ((slots, slots), (half, slots), (slots, half), (half, half))
+        ):
+            pl.when(kind == n + 1)(functools.partial(pair, q, k))
         return carry
 
-    @pl.when(flags != 0)
+    @pl.when((flags & ((1 << ri) - 1)) != 0)
     def _():
         lax.fori_loop(0, ri, body, 0)
 
@@ -122,10 +134,14 @@
         for r in range(ri):
             same = row_cluster[block * ri + r] == col_cluster[image]
             flags += same.astype(jnp.int32) * (1 << r)
+            few = row_counts[block * ri + r] <= slots // 2
+            flags += few.astype(jnp.int32) * (1 << (ri + r))
             meta[pl.ds(step * ri + r, 1), :] = jnp.full(
                 (1, slots), row_counts[block * ri + r], jnp.int32
             )
         meta[pl.ds(COLS + step, 1), :] = jnp.full((1, slots), col_counts[image], jnp.int32)
+        few = col_counts[image] <= slots // 2
+        flags += few.astype(jnp.int32) * (1 << (2 * ri))
         meta[pl.ds(FLAGS + step, 1), :] = jnp.full((1, slots), flags, jnp.int32)
     panel(0, rows, packed.at[0], meta, out)
 

time: 67.4 us -> 67.4 us (level)
  no operation moved by 1% of the time
where the time goes in v5:
time: 67.4 us; the launch traced here: 67 us
  waiting for transfers between devices  33.3 us (49%)
  starting transfers between devices  25.3 us (38%)
  Pallas kernels  8.37 us (12%)
    ppermute x7, waiting for transfers between devices, move(): return lax.ppermute(value, ('row', 'col'), perm)  33.3 us
    ppermute x7, starting transfers between devices, move(): return lax.ppermute(value, ('row', 'col'), perm)  25.3 us
    pallas_call x1, Pallas kernels, local(): pl.pallas_call(fourth_kernel, out_shape=whole, in_specs=[VMEM] * 5, out_s...  1.88 us
    pallas_call x1, Pallas kernels, local(): pl.pallas_call(middle_kernel, out_shape=many(3), in_specs=[VMEM] * 5, out...  1.87 us
  transfers between devices with their start and end apart: 7, of which 5 were waited for; matrix products, arithmetic and copies ran while one was open for 0% of the time, Pallas kernels for 10%

profile of v5, /device:TPU:24, one launch (start us, length us, event | category | flops | bytes accessed | tf_op | source)
XLA Modules:
  0.0 67.0 jit_solution(9097797770219474208)
XLA Ops:
  0.0 0.0 copy-start
  0.0 4.8 %collective-permute-start = (bf16[4,256,256]{2,1,0:T(8,128)(2,1)}, bf16[4,256,256]{2,1,0:T(8,128)(2,1)S(1)}, u32[]{:S(2)}, u32[]{:S(2)}) collective-permute-start(bf16[4,256,256]{2,1,0:T(8,128)(2,1)} %rows0.3), channel_id=1, source_target_pairs={{0,2},{1,3},{2,4},{3,5},{4,6},{5,7},{6,8},{7,9},{8,10},{9,11},{10,... | collective-permute-start | bytes 1572872 | tf_op jit(solution)/shard_map/ppermute | solution.py:30
  4.8 11.5 %collective-permute-done.rows2 = bf16[4,256,256]{2,1,0:T(8,128)(2,1)S(1)} collective-permute-done((bf16[4,256,256]{2,1,0:T(8,128)(2,1)}, bf16[4,256,256]{2,1,0:T(8,128)(2,1)S(1)}, u32[]{:S(2)}, u32[]{:S(2)}) %collective-permute-start) | collective-permute-done | bytes 524320 | tf_op jit(solution)/shard_map/ppermute | solution.py:30
  16.3 5.5 %collective-permute-start.1 = (bf16[4,256,256]{2,1,0:T(8,128)(2,1)S(1)}, bf16[4,256,256]{2,1,0:T(8,128)(2,1)S(1)}, u32[]{:S(2)}, u32[]{:S(2)}) collective-permute-start(bf16[4,256,256]{2,1,0:T(8,128)(2,1)S(1)} %collective-permute-done.rows2), channel_id=1, source_target_pairs={{0,2},{1,3},{2,4},{3,5},{4,6},{5,7},{6,8},{7,9},{8,10},{9,11},{10,... | collective-permute-start | bytes 1572872 | tf_op jit(solution)/shard_map/ppermute | solution.py:30
  21.8 0.9 %pack.1.packed = bf16[1,264,256]{2,1,0:T(8,128)(2,1)S(1)} custom-call(bf16[1,256,256]{2,1,0:T(8,128)(2,1)} %col_desc.1, bf16[1,2,256]{2,1,0:T(2,128)(2,1)} %coords.1), custom_call_target="tpu_custom_call" | custom-call | tf_op jit(solution)/shard_map/pack/pallas_call | solution.py:219
  22.7 4.3 %collective-permute-start.4 = (bf16[1,264,256]{2,1,0:T(8,128)(2,1)S(1)}, bf16[1,264,256]{2,1,0:T(8,128)(2,1)S(1)}, u32[]{:S(2)}, u32[]{:S(2)}) collective-permute-start(bf16[1,264,256]{2,1,0:T(8,128)(2,1)S(1)} %pack.1.packed), channel_id=1, source_target_pairs={{0,64},{1,65},{2,66},{3,67},{4,68},{5,69},{6,70},{7,71},{8,72},{9,... | collective-permute-start | bytes 405512 | tf_op jit(solution)/shard_map/ppermute | solution.py:30
  27.0 4.9 %collective-permute-start.3 = (bf16[1,264,256]{2,1,0:T(8,128)(2,1)S(1)}, bf16[1,264,256]{2,1,0:T(8,128)(2,1)S(1)}, u32[]{:S(2)}, u32[]{:S(2)}) collective-permute-start(bf16[1,264,256]{2,1,0:T(8,128)(2,1)S(1)} %pack.1.packed), channel_id=1, source_target_pairs={{0,32},{1,33},{2,34},{3,35},{4,36},{5,37},{6,38},{7,39},{8,40},{9,... | collective-permute-start | bytes 405512 | tf_op jit(solution)/shard_map/ppermute | solution.py:30
  31.9 4.7 %collective-permute-done.4.image4.packed = bf16[1,264,256]{2,1,0:T(8,128)(2,1)S(1)} collective-permute-done((bf16[1,264,256]{2,1,0:T(8,128)(2,1)S(1)}, bf16[1,264,256]{2,1,0:T(8,128)(2,1)S(1)}, u32[]{:S(2)}, u32[]{:S(2)}) %collective-permute-start.4) | collective-permute-done | bytes 135200 | tf_op jit(solution)/shard_map/ppermute | solution.py:30
  36.6 5.3 %collective-permute-done.3.image2 = bf16[1,264,256]{2,1,0:T(8,128)(2,1)S(1)} collective-permute-done((bf16[1,264,256]{2,1,0:T(8,128)(2,1)S(1)}, bf16[1,264,256]{2,1,0:T(8,128)(2,1)S(1)}, u32[]{:S(2)}, u32[]{:S(2)}) %collective-permute-start.3) | collective-permute-done | bytes 135200 | tf_op jit(solution)/shard_map/ppermute | solution.py:30
  41.9 1.9 %collective-permute-start.5 = (bf16[2,264,256]{2,1,0:T(8,128)(2,1)S(1)}, bf16[2,264,256]{2,1,0:T(8,128)(2,1)S(1)}, u32[]{:S(2)}, u32[]{:S(2)}) collective-permute-start(bf16[2,264,256]{2,1,0:T(8,128)(2,1)S(1)} %join.1), channel_id=1, source_target_pairs={{0,31},{1,16},{2,17},{3,18},{4,19},{5,20},{6,21},{7,22},{8,23},{9,... | collective-permute-start | bytes 811016 | tf_op jit(solution)/shard_map/ppermute | solution.py:30
  43.8 1.9 %collective-permute-start.2 = (bf16[1,264,256]{2,1,0:T(8,128)(2,1)S(1)}, bf16[1,264,256]{2,1,0:T(8,128)(2,1)S(1)}, u32[]{:S(2)}, u32[]{:S(2)}) collective-permute-start(bf16[1,264,256]{2,1,0:T(8,128)(2,1)S(1)} %pack.1.packed), channel_id=1, source_target_pairs={{0,31},{1,16},{2,17},{3,18},{4,19},{5,20},{6,21},{7,22},{8,23},{9,... | collective-permute-start | bytes 405512 | tf_op jit(solution)/shard_map/ppermute | solution.py:30
  45.8 0.0 copy-done
  45.8 1.2 %first.1 = (f32[3,4,256]{2,1,0:T(4,128)S(1)}, s32[40,256]{1,0:T(8,128)S(1)}) custom-call(s32[2048]{0:T(1024)} %row_counts.1, s32[512]{0:T(512)} %col_counts.1, s32[2048]{0:T(1024)} %row_cluster.1, s32[512]{0:T(512)} %col_cluster.1, bf16[4,256,256]{2,1,0:T(8,128)(2,1)S(1)} %copy-done, bf16[1,264,256]{2,1,0:T(8,128)(2,1)S(1)} %pack.1.packed), custom_call_target="tpu_custom_call" | custom-call | tf_op jit(solution)/shard_map/first/pallas_call | solution.py:244
  47.0 8.8 %collective-permute-done.2.direct = bf16[1,264,256]{2,1,0:T(8,128)(2,1)S(1)} collective-permute-done((bf16[1,264,256]{2,1,0:T(8,128)(2,1)S(1)}, bf16[1,264,256]{2,1,0:T(8,128)(2,1)S(1)}, u32[]{:S(2)}, u32[]{:S(2)}) %collective-permute-start.2) | collective-permute-done | bytes 135200 | tf_op jit(solution)/shard_map/ppermute | solution.py:30
  55.8 0.7 %early.1 = (f32[3,4,256]{2,1,0:T(4,128)S(1)}, f32[3,3,4,256]{3,2,1,0:T(4,128)S(1)}) custom-call(s32[40,256]{1,0:T(8,128)S(1)} %get-tuple-element.9.meta, bf16[4,256,256]{2,1,0:T(8,128)(2,1)S(1)} %copy-done, bf16[4,256,256]{2,1,0:T(8,128)(2,1)S(1)} %collective-permute-done.rows2, bf16[1,264,256]{2,1,0:T(8,128)(2,1)S(1)} %collective-permute-done.3.image2, ...), custom_call_target="tpu_custom_call" | custom-call | tf_op jit(solution)/shard_map/early/pallas_call | solution.py:254
  56.5 0.0 collective-permute-done.5.images
  56.5 1.9 %middle.1.kept = f32[3,3,4,256]{3,2,1,0:T(4,128)S(1)} custom-call(s32[40,256]{1,0:T(8,128)S(1)} %get-tuple-element.9.meta, bf16[4,256,256]{2,1,0:T(8,128)(2,1)S(1)} %copy-done, bf16[4,256,256]{2,1,0:T(8,128)(2,1)S(1)} %collective-permute-done.rows2, bf16[2,264,256]{2,1,0:T(8,128)(2,1)S(1)} %collective-permute-done.5.images, ...), custom_call_target="tpu_custom_call", output_to_operand_aliasing={{}: (4, {})} | custom-call | tf_op jit(solution)/shard_map/middle/pallas_call | solution.py:261
  58.4 0.0 collective-permute-done.1.rows4.rows
  58.4 1.3 %late.1 = f32[3,3,4,256]{3,2,1,0:T(4,128)S(1)} custom-call(s32[40,256]{1,0:T(8,128)S(1)} %get-tuple-element.9.meta, bf16[4,256,256]{2,1,0:T(8,128)(2,1)S(1)} %collective-permute-done.1.rows4.rows, bf16[1,264,256]{2,1,0:T(8,128)(2,1)S(1)} %collective-permute-done.2.direct, ...), custom_call_target="tpu_custom_call", output_to_operand_aliasing={{}: (4, {})} | custom-call | tf_op jit(solution)/shard_map/late/pallas_call | solution.py:269
  59.6 1.9 %collective-permute-start.6 = (f32[3,3,4,256]{3,2,1,0:T(4,128)S(1)}, f32[3,3,4,256]{3,2,1,0:T(4,128)S(1)}, u32[]{:S(2)}, u32[]{:S(2)}) collective-permute-start(f32[3,3,4,256]{3,2,1,0:T(4,128)S(1)} %late.1), channel_id=1, source_target_pairs={{0,1},{1,2},{2,3},{3,4},{4,5},{5,6},{6,7},{7,8},{8,9},{9,10},{10,1... | collective-permute-start | bytes 110600 | tf_op jit(solution)/shard_map/ppermute | solution.py:30
  61.5 1.9 %fourth.1.kept = f32[6,3,4,256]{3,2,1,0:T(4,128)} custom-call(s32[40,256]{1,0:T(8,128)S(1)} %get-tuple-element.9.meta, bf16[4,256,256]{2,1,0:T(8,128)(2,1)S(1)} %collective-permute-done.1.rows4.rows, bf16[1,264,256]{2,1,0:T(8,128)(2,1)S(1)} %collective-permute-done.4.image4.packed, f32[3,4,256]{2,1,0:T(4,128)S(1)} %get-tuple-element.11.res0, ...), custom_call_target="tpu_custom_call" | custom-call | tf_op jit(solution)/shard_map/fourth/pallas_call | solution.py:280
  63.4 2.9 %collective-permute-done.6.home = f32[3,3,4,256]{3,2,1,0:T(4,128)S(1)} collective-permute-done((f32[3,3,4,256]{3,2,1,0:T(4,128)S(1)}, f32[3,3,4,256]{3,2,1,0:T(4,128)S(1)}, u32[]{:S(2)}, u32[]{:S(2)}) %collective-permute-start.6) | collective-permute-done | bytes 36896 | tf_op jit(solution)/shard_map/ppermute | solution.py:30
  66.4 0.6 final.1
  (1 shorter events, 0.0 us)
Async XLA Ops:
  0.0 45.8 %copy-start = (bf16[4,256,256]{2,1,0:T(8,128)(2,1)S(1)}, bf16[4,256,256]{2,1,0:T(8,128)(2,1)}, u32[]{:S(2)}) copy-start(bf16[4,256,256]{2,1,0:T(8,128)(2,1)} %rows0.3) | copy-start | bytes 1572868
  0.0 16.3 %collective-permute-start = (bf16[4,256,256]{2,1,0:T(8,128)(2,1)}, bf16[4,256,256]{2,1,0:T(8,128)(2,1)S(1)}, u32[]{:S(2)}, u32[]{:S(2)}) collective-permute-start(bf16[4,256,256]{2,1,0:T(8,128)(2,1)} %rows0.3), channel_id=1, source_target_pairs={{0,2},{1,3},{2,4},{3,5},{4,6},{5,7},{6,8},{7,9},{8,10},{9,11},{10,... | collective-permute-start | bytes 1572872 | tf_op jit(solution)/shard_map/ppermute | solution.py:30
  16.3 42.1 %collective-permute-start.1 = (bf16[4,256,256]{2,1,0:T(8,128)(2,1)S(1)}, bf16[4,256,256]{2,1,0:T(8,128)(2,1)S(1)}, u32[]{:S(2)}, u32[]{:S(2)}) collective-permute-start(bf16[4,256,256]{2,1,0:T(8,128)(2,1)S(1)} %collective-permute-done.rows2), channel_id=1, source_target_pairs={{0,2},{1,3},{2,4},{3,5},{4,6},{5,7},{6,8},{7,9},{8,10},{9,11},{10,... | collective-permute-start | bytes 1572872 | tf_op jit(solution)/shard_map/ppermute | solution.py:30
  22.7 13.9 %collective-permute-start.4 = (bf16[1,264,256]{2,1,0:T(8,128)(2,1)S(1)}, bf16[1,264,256]{2,1,0:T(8,128)(2,1)S(1)}, u32[]{:S(2)}, u32[]{:S(2)}) collective-permute-start(bf16[1,264,256]{2,1,0:T(8,128)(2,1)S(1)} %pack.1.packed), channel_id=1, source_target_pairs={{0,64},{1,65},{2,66},{3,67},{4,68},{5,69},{6,70},{7,71},{8,72},{9,... | collective-permute-start | bytes 405512 | tf_op jit(solution)/shard_map/ppermute | solution.py:30
  27.0 14.9 %collective-permute-start.3 = (bf16[1,264,256]{2,1,0:T(8,128)(2,1)S(1)}, bf16[1,264,256]{2,1,0:T(8,128)(2,1)S(1)}, u32[]{:S(2)}, u32[]{:S(2)}) collective-permute-start(bf16[1,264,256]{2,1,0:T(8,128)(2,1)S(1)} %pack.1.packed), channel_id=1, source_target_pairs={{0,32},{1,33},{2,34},{3,35},{4,36},{5,37},{6,38},{7,39},{8,40},{9,... | collective-permute-start | bytes 405512 | tf_op jit(solution)/shard_map/ppermute | solution.py:30
  41.9 14.6 %collective-permute-start.5 = (bf16[2,264,256]{2,1,0:T(8,128)(2,1)S(1)}, bf16[2,264,256]{2,1,0:T(8,128)(2,1)S(1)}, u32[]{:S(2)}, u32[]{:S(2)}) collective-permute-start(bf16[2,264,256]{2,1,0:T(8,128)(2,1)S(1)} %join.1), channel_id=1, source_target_pairs={{0,31},{1,16},{2,17},{3,18},{4,19},{5,20},{6,21},{7,22},{8,23},{9,... | collective-permute-start | bytes 811016 | tf_op jit(solution)/shard_map/ppermute | solution.py:30
  43.8 12.0 %collective-permute-start.2 = (bf16[1,264,256]{2,1,0:T(8,128)(2,1)S(1)}, bf16[1,264,256]{2,1,0:T(8,128)(2,1)S(1)}, u32[]{:S(2)}, u32[]{:S(2)}) collective-permute-start(bf16[1,264,256]{2,1,0:T(8,128)(2,1)S(1)} %pack.1.packed), channel_id=1, source_target_pairs={{0,31},{1,16},{2,17},{3,18},{4,19},{5,20},{6,21},{7,22},{8,23},{9,... | collective-permute-start | bytes 405512 | tf_op jit(solution)/shard_map/ppermute | solution.py:30
  59.6 6.7 %collective-permute-start.6 = (f32[3,3,4,256]{3,2,1,0:T(4,128)S(1)}, f32[3,3,4,256]{3,2,1,0:T(4,128)S(1)}, u32[]{:S(2)}, u32[]{:S(2)}) collective-permute-start(f32[3,3,4,256]{3,2,1,0:T(4,128)S(1)} %late.1), channel_id=1, source_target_pairs={{0,1},{1,2},{2,3},{3,4},{4,5},{5,6},{6,7},{7,8},{8,9},{9,10},{10,1... | collective-permute-start | bytes 110600 | tf_op jit(solution)/shard_map/ppermute | solution.py:30

commit v6 on v4

--- a/solution.py
+++ b/solution.py
@@ -14,6 +14,7 @@
 COLS = 24
 FLAGS = 32
 inv_temp = 10.0
+log2_e = 1.4426950408889634
 big_value = 1e30
 
 SMEM = pl.BlockSpec(memory_space=pltpu.SMEM)
@@ -36,15 +37,15 @@
 
 def one_pair(rows, packed, row_count, col_count):
     k = packed.shape[0] - TABLE
-    scores = inv_temp * lax.dot_general(
+    scores = (inv_temp * log2_e) * lax.dot_general(
         packed[:k], rows, (((1,), (1,)), ((), ())), preferred_element_type=jnp.float32
     )
     col_ok = lax.broadcasted_iota(jnp.int32, scores.shape, 0) < col_count
     row_ok = lax.broadcasted_iota(jnp.int32, (1, scores.shape[1]), 1) < row_count
     over_col = jnp.where(col_ok, scores, -big_value)
     over_row = jnp.where(row_ok, scores, -big_value)
-    row_exp = jnp.exp(over_col - jnp.max(over_col, axis=0, keepdims=True))
-    col_exp = jnp.exp(over_row - jnp.max(over_row, axis=1, keepdims=True))
+    row_exp = jnp.exp2(over_col - jnp.max(over_col, axis=0, keepdims=True))
+    col_exp = jnp.exp2(over_row - jnp.max(over_row, axis=1, keepdims=True))
     row_inv = 1.0 / jnp.sum(row_exp, axis=0, keepdims=True)
     col_inv = 1.0 / jnp.sum(col_exp, axis=1, keepdims=True)
     prob = ((row_exp * row_inv) * (col_exp * col_inv)).astype(jnp.bfloat16)

time: 67.4 us -> 67.4 us (level)
  no operation moved by 1% of the time
where the time goes in v6:
time: 67.4 us; the launch traced here: 67 us
  waiting for transfers between devices  33.3 us (49%)
  starting transfers between devices  25.3 us (38%)
  Pallas kernels  8.32 us (12%)
    ppermute x7, waiting for transfers between devices, move(): return lax.ppermute(value, ('row', 'col'), perm)  33.3 us
    ppermute x7, starting transfers between devices, move(): return lax.ppermute(value, ('row', 'col'), perm)  25.3 us
    pallas_call x1, Pallas kernels, local(): pl.pallas_call(middle_kernel, out_shape=many(3), in_specs=[VMEM] * 5, out...  1.9 us
    pallas_call x1, Pallas kernels, local(): pl.pallas_call(fourth_kernel, out_shape=whole, in_specs=[VMEM] * 5, out_s...  1.85 us
  transfers between devices with their start and end apart: 7, of which 5 were waited for; matrix products, arithmetic and copies ran while one was open for 0% of the time, Pallas kernels for 10%

profile of v6, /device:TPU:24, one launch (start us, length us, event | category | flops | bytes accessed | tf_op | source)
XLA Modules:
  0.0 67.0 jit_solution(4494958567388992511)
XLA Ops:
  0.0 0.0 copy-start
  0.0 4.8 %collective-permute-start = (bf16[4,256,256]{2,1,0:T(8,128)(2,1)}, bf16[4,256,256]{2,1,0:T(8,128)(2,1)S(1)}, u32[]{:S(2)}, u32[]{:S(2)}) collective-permute-start(bf16[4,256,256]{2,1,0:T(8,128)(2,1)} %rows0.3), channel_id=1, source_target_pairs={{0,2},{1,3},{2,4},{3,5},{4,6},{5,7},{6,8},{7,9},{8,10},{9,11},{10,... | collective-permute-start | bytes 1572872 | tf_op jit(solution)/shard_map/ppermute | solution.py:31
  4.8 11.5 %collective-permute-done.rows2 = bf16[4,256,256]{2,1,0:T(8,128)(2,1)S(1)} collective-permute-done((bf16[4,256,256]{2,1,0:T(8,128)(2,1)}, bf16[4,256,256]{2,1,0:T(8,128)(2,1)S(1)}, u32[]{:S(2)}, u32[]{:S(2)}) %collective-permute-start) | collective-permute-done | bytes 524320 | tf_op jit(solution)/shard_map/ppermute | solution.py:31
  16.3 5.5 %collective-permute-start.1 = (bf16[4,256,256]{2,1,0:T(8,128)(2,1)S(1)}, bf16[4,256,256]{2,1,0:T(8,128)(2,1)S(1)}, u32[]{:S(2)}, u32[]{:S(2)}) collective-permute-start(bf16[4,256,256]{2,1,0:T(8,128)(2,1)S(1)} %collective-permute-done.rows2), channel_id=1, source_target_pairs={{0,2},{1,3},{2,4},{3,5},{4,6},{5,7},{6,8},{7,9},{8,10},{9,11},{10,... | collective-permute-start | bytes 1572872 | tf_op jit(solution)/shard_map/ppermute | solution.py:31
  21.8 0.9 %pack.1.packed = bf16[1,264,256]{2,1,0:T(8,128)(2,1)S(1)} custom-call(bf16[1,256,256]{2,1,0:T(8,128)(2,1)} %col_desc.1, bf16[1,2,256]{2,1,0:T(2,128)(2,1)} %coords.1), custom_call_target="tpu_custom_call" | custom-call | tf_op jit(solution)/shard_map/pack/pallas_call | solution.py:204
  22.7 4.3 %collective-permute-start.4 = (bf16[1,264,256]{2,1,0:T(8,128)(2,1)S(1)}, bf16[1,264,256]{2,1,0:T(8,128)(2,1)S(1)}, u32[]{:S(2)}, u32[]{:S(2)}) collective-permute-start(bf16[1,264,256]{2,1,0:T(8,128)(2,1)S(1)} %pack.1.packed), channel_id=1, source_target_pairs={{0,64},{1,65},{2,66},{3,67},{4,68},{5,69},{6,70},{7,71},{8,72},{9,... | collective-permute-start | bytes 405512 | tf_op jit(solution)/shard_map/ppermute | solution.py:31
  27.0 4.9 %collective-permute-start.3 = (bf16[1,264,256]{2,1,0:T(8,128)(2,1)S(1)}, bf16[1,264,256]{2,1,0:T(8,128)(2,1)S(1)}, u32[]{:S(2)}, u32[]{:S(2)}) collective-permute-start(bf16[1,264,256]{2,1,0:T(8,128)(2,1)S(1)} %pack.1.packed), channel_id=1, source_target_pairs={{0,32},{1,33},{2,34},{3,35},{4,36},{5,37},{6,38},{7,39},{8,40},{9,... | collective-permute-start | bytes 405512 | tf_op jit(solution)/shard_map/ppermute | solution.py:31
  31.9 4.7 %collective-permute-done.4.image4.packed = bf16[1,264,256]{2,1,0:T(8,128)(2,1)S(1)} collective-permute-done((bf16[1,264,256]{2,1,0:T(8,128)(2,1)S(1)}, bf16[1,264,256]{2,1,0:T(8,128)(2,1)S(1)}, u32[]{:S(2)}, u32[]{:S(2)}) %collective-permute-start.4) | collective-permute-done | bytes 135200 | tf_op jit(solution)/shard_map/ppermute | solution.py:31
  36.6 5.3 %collective-permute-done.3.image2 = bf16[1,264,256]{2,1,0:T(8,128)(2,1)S(1)} collective-permute-done((bf16[1,264,256]{2,1,0:T(8,128)(2,1)S(1)}, bf16[1,264,256]{2,1,0:T(8,128)(2,1)S(1)}, u32[]{:S(2)}, u32[]{:S(2)}) %collective-permute-start.3) | collective-permute-done | bytes 135200 | tf_op jit(solution)/shard_map/ppermute | solution.py:31
  41.9 1.9 %collective-permute-start.5 = (bf16[2,264,256]{2,1,0:T(8,128)(2,1)S(1)}, bf16[2,264,256]{2,1,0:T(8,128)(2,1)S(1)}, u32[]{:S(2)}, u32[]{:S(2)}) collective-permute-start(bf16[2,264,256]{2,1,0:T(8,128)(2,1)S(1)} %join.1), channel_id=1, source_target_pairs={{0,31},{1,16},{2,17},{3,18},{4,19},{5,20},{6,21},{7,22},{8,23},{9,... | collective-permute-start | bytes 811016 | tf_op jit(solution)/shard_map/ppermute | solution.py:31
  43.8 1.9 %collective-permute-start.2 = (bf16[1,264,256]{2,1,0:T(8,128)(2,1)S(1)}, bf16[1,264,256]{2,1,0:T(8,128)(2,1)S(1)}, u32[]{:S(2)}, u32[]{:S(2)}) collective-permute-start(bf16[1,264,256]{2,1,0:T(8,128)(2,1)S(1)} %pack.1.packed), channel_id=1, source_target_pairs={{0,31},{1,16},{2,17},{3,18},{4,19},{5,20},{6,21},{7,22},{8,23},{9,... | collective-permute-start | bytes 405512 | tf_op jit(solution)/shard_map/ppermute | solution.py:31
  45.8 0.0 copy-done
  45.8 1.2 %first.1 = (f32[3,4,256]{2,1,0:T(4,128)S(1)}, s32[40,256]{1,0:T(8,128)S(1)}) custom-call(s32[2048]{0:T(1024)} %row_counts.1, s32[512]{0:T(512)} %col_counts.1, s32[2048]{0:T(1024)} %row_cluster.1, s32[512]{0:T(512)} %col_cluster.1, bf16[4,256,256]{2,1,0:T(8,128)(2,1)S(1)} %copy-done, bf16[1,264,256]{2,1,0:T(8,128)(2,1)S(1)} %pack.1.packed), custom_call_target="tpu_custom_call" | custom-call | tf_op jit(solution)/shard_map/first/pallas_call | solution.py:229
  47.0 8.9 %collective-permute-done.2.direct = bf16[1,264,256]{2,1,0:T(8,128)(2,1)S(1)} collective-permute-done((bf16[1,264,256]{2,1,0:T(8,128)(2,1)S(1)}, bf16[1,264,256]{2,1,0:T(8,128)(2,1)S(1)}, u32[]{:S(2)}, u32[]{:S(2)}) %collective-permute-start.2) | collective-permute-done | bytes 135200 | tf_op jit(solution)/shard_map/ppermute | solution.py:31
  55.8 0.7 %early.1 = (f32[3,4,256]{2,1,0:T(4,128)S(1)}, f32[3,3,4,256]{3,2,1,0:T(4,128)S(1)}) custom-call(s32[40,256]{1,0:T(8,128)S(1)} %get-tuple-element.9.meta, bf16[4,256,256]{2,1,0:T(8,128)(2,1)S(1)} %copy-done, bf16[4,256,256]{2,1,0:T(8,128)(2,1)S(1)} %collective-permute-done.rows2, bf16[1,264,256]{2,1,0:T(8,128)(2,1)S(1)} %collective-permute-done.3.image2, ...), custom_call_target="tpu_custom_call" | custom-call | tf_op jit(solution)/shard_map/early/pallas_call | solution.py:239
  56.5 0.0 collective-permute-done.5.images
  56.5 1.9 %middle.1.kept = f32[3,3,4,256]{3,2,1,0:T(4,128)S(1)} custom-call(s32[40,256]{1,0:T(8,128)S(1)} %get-tuple-element.9.meta, bf16[4,256,256]{2,1,0:T(8,128)(2,1)S(1)} %copy-done, bf16[4,256,256]{2,1,0:T(8,128)(2,1)S(1)} %collective-permute-done.rows2, bf16[2,264,256]{2,1,0:T(8,128)(2,1)S(1)} %collective-permute-done.5.images, ...), custom_call_target="tpu_custom_call", output_to_operand_aliasing={{}: (4, {})} | custom-call | tf_op jit(solution)/shard_map/middle/pallas_call | solution.py:246
  58.4 0.0 collective-permute-done.1.rows4.rows
  58.4 1.2 %late.1 = f32[3,3,4,256]{3,2,1,0:T(4,128)S(1)} custom-call(s32[40,256]{1,0:T(8,128)S(1)} %get-tuple-element.9.meta, bf16[4,256,256]{2,1,0:T(8,128)(2,1)S(1)} %collective-permute-done.1.rows4.rows, bf16[1,264,256]{2,1,0:T(8,128)(2,1)S(1)} %collective-permute-done.2.direct, ...), custom_call_target="tpu_custom_call", output_to_operand_aliasing={{}: (4, {})} | custom-call | tf_op jit(solution)/shard_map/late/pallas_call | solution.py:254
  59.6 1.9 %collective-permute-start.6 = (f32[3,3,4,256]{3,2,1,0:T(4,128)S(1)}, f32[3,3,4,256]{3,2,1,0:T(4,128)S(1)}, u32[]{:S(2)}, u32[]{:S(2)}) collective-permute-start(f32[3,3,4,256]{3,2,1,0:T(4,128)S(1)} %late.1), channel_id=1, source_target_pairs={{0,1},{1,2},{2,3},{3,4},{4,5},{5,6},{6,7},{7,8},{8,9},{9,10},{10,1... | collective-permute-start | bytes 110600 | tf_op jit(solution)/shard_map/ppermute | solution.py:31
  61.5 1.9 %fourth.1.kept = f32[6,3,4,256]{3,2,1,0:T(4,128)} custom-call(s32[40,256]{1,0:T(8,128)S(1)} %get-tuple-element.9.meta, bf16[4,256,256]{2,1,0:T(8,128)(2,1)S(1)} %collective-permute-done.1.rows4.rows, bf16[1,264,256]{2,1,0:T(8,128)(2,1)S(1)} %collective-permute-done.4.image4.packed, f32[3,4,256]{2,1,0:T(4,128)S(1)} %get-tuple-element.11.res0, ...), custom_call_target="tpu_custom_call" | custom-call | tf_op jit(solution)/shard_map/fourth/pallas_call | solution.py:265
  63.4 3.0 %collective-permute-done.6.home = f32[3,3,4,256]{3,2,1,0:T(4,128)S(1)} collective-permute-done((f32[3,3,4,256]{3,2,1,0:T(4,128)S(1)}, f32[3,3,4,256]{3,2,1,0:T(4,128)S(1)}, u32[]{:S(2)}, u32[]{:S(2)}) %collective-permute-start.6) | collective-permute-done | bytes 36896 | tf_op jit(solution)/shard_map/ppermute | solution.py:31
  66.4 0.6 final.1
  (1 shorter events, 0.0 us)
Async XLA Ops:
  0.0 45.8 %copy-start = (bf16[4,256,256]{2,1,0:T(8,128)(2,1)S(1)}, bf16[4,256,256]{2,1,0:T(8,128)(2,1)}, u32[]{:S(2)}) copy-start(bf16[4,256,256]{2,1,0:T(8,128)(2,1)} %rows0.3) | copy-start | bytes 1572868
  0.0 16.3 %collective-permute-start = (bf16[4,256,256]{2,1,0:T(8,128)(2,1)}, bf16[4,256,256]{2,1,0:T(8,128)(2,1)S(1)}, u32[]{:S(2)}, u32[]{:S(2)}) collective-permute-start(bf16[4,256,256]{2,1,0:T(8,128)(2,1)} %rows0.3), channel_id=1, source_target_pairs={{0,2},{1,3},{2,4},{3,5},{4,6},{5,7},{6,8},{7,9},{8,10},{9,11},{10,... | collective-permute-start | bytes 1572872 | tf_op jit(solution)/shard_map/ppermute | solution.py:31
  16.3 42.1 %collective-permute-start.1 = (bf16[4,256,256]{2,1,0:T(8,128)(2,1)S(1)}, bf16[4,256,256]{2,1,0:T(8,128)(2,1)S(1)}, u32[]{:S(2)}, u32[]{:S(2)}) collective-permute-start(bf16[4,256,256]{2,1,0:T(8,128)(2,1)S(1)} %collective-permute-done.rows2), channel_id=1, source_target_pairs={{0,2},{1,3},{2,4},{3,5},{4,6},{5,7},{6,8},{7,9},{8,10},{9,11},{10,... | collective-permute-start | bytes 1572872 | tf_op jit(solution)/shard_map/ppermute | solution.py:31
  22.7 13.9 %collective-permute-start.4 = (bf16[1,264,256]{2,1,0:T(8,128)(2,1)S(1)}, bf16[1,264,256]{2,1,0:T(8,128)(2,1)S(1)}, u32[]{:S(2)}, u32[]{:S(2)}) collective-permute-start(bf16[1,264,256]{2,1,0:T(8,128)(2,1)S(1)} %pack.1.packed), channel_id=1, source_target_pairs={{0,64},{1,65},{2,66},{3,67},{4,68},{5,69},{6,70},{7,71},{8,72},{9,... | collective-permute-start | bytes 405512 | tf_op jit(solution)/shard_map/ppermute | solution.py:31
  27.0 14.9 %collective-permute-start.3 = (bf16[1,264,256]{2,1,0:T(8,128)(2,1)S(1)}, bf16[1,264,256]{2,1,0:T(8,128)(2,1)S(1)}, u32[]{:S(2)}, u32[]{:S(2)}) collective-permute-start(bf16[1,264,256]{2,1,0:T(8,128)(2,1)S(1)} %pack.1.packed), channel_id=1, source_target_pairs={{0,32},{1,33},{2,34},{3,35},{4,36},{5,37},{6,38},{7,39},{8,40},{9,... | collective-permute-start | bytes 405512 | tf_op jit(solution)/shard_map/ppermute | solution.py:31
  41.9 14.6 %collective-permute-start.5 = (bf16[2,264,256]{2,1,0:T(8,128)(2,1)S(1)}, bf16[2,264,256]{2,1,0:T(8,128)(2,1)S(1)}, u32[]{:S(2)}, u32[]{:S(2)}) collective-permute-start(bf16[2,264,256]{2,1,0:T(8,128)(2,1)S(1)} %join.1), channel_id=1, source_target_pairs={{0,31},{1,16},{2,17},{3,18},{4,19},{5,20},{6,21},{7,22},{8,23},{9,... | collective-permute-start | bytes 811016 | tf_op jit(solution)/shard_map/ppermute | solution.py:31
  43.8 12.0 %collective-permute-start.2 = (bf16[1,264,256]{2,1,0:T(8,128)(2,1)S(1)}, bf16[1,264,256]{2,1,0:T(8,128)(2,1)S(1)}, u32[]{:S(2)}, u32[]{:S(2)}) collective-permute-start(bf16[1,264,256]{2,1,0:T(8,128)(2,1)S(1)} %pack.1.packed), channel_id=1, source_target_pairs={{0,31},{1,16},{2,17},{3,18},{4,19},{5,20},{6,21},{7,22},{8,23},{9,... | collective-permute-start | bytes 405512 | tf_op jit(solution)/shard_map/ppermute | solution.py:31
  59.6 6.7 %collective-permute-start.6 = (f32[3,3,4,256]{3,2,1,0:T(4,128)S(1)}, f32[3,3,4,256]{3,2,1,0:T(4,128)S(1)}, u32[]{:S(2)}, u32[]{:S(2)}) collective-permute-start(f32[3,3,4,256]{3,2,1,0:T(4,128)S(1)} %late.1), channel_id=1, source_target_pairs={{0,1},{1,2},{2,3},{3,4},{4,5},{5,6},{6,7},{7,8},{8,9},{9,10},{10,1... | collective-permute-start | bytes 110600 | tf_op jit(solution)/shard_map/ppermute | solution.py:31
